TPU v7x, 512 devices: a whole 4x8x8 slice. The times are simulated.
512 devices in a mesh: gx: 4 (over x), gy: 8 (over y), goal: 16 (over z, core).
Axes of the slice: x: 4, y: 8, z: 8, core: 2. Of those that a mesh axis runs over, the one named last changes fastest.
Arguments:
- potential: float32 [64, 512, 2048], P('goal', 'gx', 'gy'), as said below
- cost: float32 [512, 2048], P('gx', 'gy'), may hold values from 1 to 3
- obstacle: int32 [512, 2048], P('gx', 'gy'), may hold values 0 or 1
- density: float32 [4, 512, 2048], P(None, 'gx', 'gy'), may hold values from 0.1 to 1
- destinations: int32 [64], P('goal'), may hold values from 0 to 1048575, as said below
- group_ids: int32 [64], P('goal'), may hold values from 0 to 3, as said below
Outputs:
- potential_out: float32 [64, 512, 2048], P('goal', 'gx', 'gy')
- velocity: float32 [4, 2, 512, 2048], P(None, None, 'gx', 'gy')
- density_out: float32 [4, 512, 2048], P(None, 'gx', 'gy')
Inputs may be any that keep to these rules, and one draw needn't show every extreme that they name: `potential`: potentials are non-negative. `destinations`: row * 2048 + column of the destination cell. `group_ids`: every group serves at least one destination.
All inputs are finite; a program needn't handle non-finite values. No bound on the sum of `obstacle` on one device may be relied on, other than what follows from the above.
Results may differ from a plain program's by a relative error of at most 0.0003.
Values sent between devices are 32-bit elements; how exact they have to be, the bound alone decides.
A program may use at most 64 MiB of HBM per device.

v0:
```python
from functools import reduce

import jax
import jax.numpy as jnp
from jax import lax
from jax.sharding import PartitionSpec as P

SWEEPS = 8


CELL_SIZE = 0.005
SWEEP_TEMP = 0.002
GOAL_TEMP = 0.01
OBSTACLE_COST = 8.0
COURANT = 0.4
FAR_VALUE = 10000.0
NEG_FILL = -1e30


def extended_2(cells, sides, width):
    for axis, dim in sides:
        count = lax.axis_size(axis)
        ends = count - 1
        head = lax.slice_in_dim(cells, 0, width, axis=dim)
        tail = lax.slice_in_dim(cells, cells.shape[dim] - width, cells.shape[dim], axis=dim)
        cells = jnp.concatenate(
            [
                lax.ppermute(tail, axis, [(i, (i + 1) % count) for i in range(ends)]),
                cells,
                lax.ppermute(head, axis, [((i + 1) % count, i) for i in range(ends)]),
            ],
            axis=dim,
        )
    return cells


def relax_sweep(extended, inside_ext, step_cost, pinned):
    centre = extended[..., 1:-1, 1:-1]
    candidates = [centre]
    pairs = (
        (extended[..., :-2, 1:-1], inside_ext[:-2, 1:-1]),
        (extended[..., 2:, 1:-1], inside_ext[2:, 1:-1]),
        (extended[..., 1:-1, :-2], inside_ext[1:-1, :-2]),
        (extended[..., 1:-1, 2:], inside_ext[1:-1, 2:]),
    )
    for beside, valid in pairs:
        candidates.append(jnp.where(valid, beside + step_cost, FAR_VALUE))
    lowest = reduce(jnp.minimum, candidates)
    weight_sum = reduce(jnp.add, [jnp.exp((lowest - item) / SWEEP_TEMP) for item in candidates])
    return jnp.where(pinned, 0.0, lowest - SWEEP_TEMP * jnp.log(weight_sum))


def advect_step(field_two, density_one, inside_two):
    centre = field_two[:, 1:-1, 1:-1]
    north_value = jnp.where(inside_two[:-2, 1:-1], field_two[:, :-2, 1:-1], centre)
    south_value = jnp.where(inside_two[2:, 1:-1], field_two[:, 2:, 1:-1], centre)
    west_value = jnp.where(inside_two[1:-1, :-2], field_two[:, 1:-1, :-2], centre)
    east_value = jnp.where(inside_two[1:-1, 2:], field_two[:, 1:-1, 2:], centre)
    grad_x = (south_value - north_value) / (2.0 * CELL_SIZE)
    grad_y = (east_value - west_value) / (2.0 * CELL_SIZE)
    speed_factor = 1.0 / (1.0 + jnp.sum(density_one, axis=0))
    scale_factor = speed_factor / jnp.sqrt(1.0 + grad_x * grad_x + grad_y * grad_y)
    flow_x = -scale_factor * grad_x
    flow_y = -scale_factor * grad_y
    inside_one = inside_two[1:-1, 1:-1]
    face_x = 0.5 * (flow_x[:, :-1, 1:-1] + flow_x[:, 1:, 1:-1])
    flux_x = (
        jnp.maximum(face_x, 0.0) * density_one[:, :-1, 1:-1]
        + jnp.minimum(face_x, 0.0) * density_one[:, 1:, 1:-1]
    )
    flux_x = jnp.where(inside_one[:-1, 1:-1] & inside_one[1:, 1:-1], flux_x, 0.0)
    face_y = 0.5 * (flow_y[:, 1:-1, :-1] + flow_y[:, 1:-1, 1:])
    flux_y = (
        jnp.maximum(face_y, 0.0) * density_one[:, 1:-1, :-1]
        + jnp.minimum(face_y, 0.0) * density_one[:, 1:-1, 1:]
    )
    flux_y = jnp.where(inside_one[1:-1, :-1] & inside_one[1:-1, 1:], flux_y, 0.0)
    updated = density_one[:, 1:-1, 1:-1] - COURANT * (
        flux_x[:, 1:] - flux_x[:, :-1] + flux_y[:, :, 1:] - flux_y[:, :, :-1]
    )
    velocity = jnp.stack((flow_x[:, 1:-1, 1:-1], flow_y[:, 1:-1, 1:-1]), axis=1)
    return (velocity, updated)


def region(row_start, col_start, nx_all, ny_all, height, width, cycle_width, dest_rows, dest_cols):
    row_index = row_start - cycle_width + jnp.arange(height + 2 * cycle_width, dtype=jnp.int32)
    col_index = col_start - cycle_width + jnp.arange(width + 2 * cycle_width, dtype=jnp.int32)
    inside = ((row_index >= 0) & (row_index < nx_all))[:, None] & (
        (col_index >= 0) & (col_index < ny_all)
    )[None, :]
    pinned = (row_index[None, :, None] == dest_rows[:, None, None]) & (
        col_index[None, None, :] == dest_cols[:, None, None]
    )
    return (inside, pinned)


def goal_soft_min(field_now, group_ids, groups):
    scores = -field_now / GOAL_TEMP
    member = (group_ids[:, None] == jnp.arange(groups, dtype=jnp.int32)[None, :])[:, :, None, None]
    masked = jnp.where(member, scores[:, None], NEG_FILL)
    peak_score = jnp.max(masked, axis=0)
    peak_score = lax.pmax(peak_score, "goal")
    local_sum = jnp.sum(jnp.where(member, jnp.exp(scores[:, None] - peak_score[None]), 0.0), axis=0)
    weight_sum = lax.psum(local_sum, "goal")
    return -GOAL_TEMP * (peak_score + jnp.log(weight_sum))


def per_device(potential, cost, obstacle, density, destinations, group_ids):
    goal_count, height, width = potential.shape
    groups = density.shape[0]
    nx_all = height * lax.axis_size("gx")
    ny_all = width * lax.axis_size("gy")
    row_start = lax.axis_index("gx") * height
    col_start = lax.axis_index("gy") * width
    dest_rows = destinations // ny_all
    dest_cols = destinations % ny_all
    cost_full = cost + OBSTACLE_COST * obstacle.astype(jnp.float32)
    inside_one = region(
        row_start, col_start, nx_all, ny_all, height, width, 1, dest_rows, dest_cols
    )[0]
    pinned = region(row_start, col_start, nx_all, ny_all, height, width, 0, dest_rows, dest_cols)[1]
    step_cost = cost_full * CELL_SIZE
    field_now = potential
    for sweep_index in range(SWEEPS):
        extended = extended_2(field_now, (("gx", 1), ("gy", 2)), 1)
        field_now = relax_sweep(extended, inside_one, step_cost, pinned)
    group_field = goal_soft_min(field_now, group_ids, groups)
    stacked = jnp.concatenate((group_field, density), axis=0)
    grown = extended_2(stacked, (("gx", 1), ("gy", 2)), 2)
    field_two = grown[:groups]
    density_one = grown[groups:, 1:-1, 1:-1]
    inside_two = region(
        row_start, col_start, nx_all, ny_all, height, width, 2, dest_rows, dest_cols
    )[0]
    velocity, density_out = advect_step(field_two, density_one, inside_two)
    return (field_now, velocity, density_out)


def solution(mesh):
    in_specs = (
        P("goal", "gx", "gy"),
        P("gx", "gy"),
        P("gx", "gy"),
        P(None, "gx", "gy"),
        P("goal"),
        P("goal"),
    )
    out_specs = (P("goal", "gx", "gy"), P(None, None, "gx", "gy"), P(None, "gx", "gy"))
    return jax.shard_map(
        per_device, mesh=mesh, in_specs=in_specs, out_specs=out_specs, check_vma=False
    )
```

profile of v0, /device:TPU:1, one launch (start us, length us, event | category | flops | bytes accessed | tf_op | source)
XLA Modules:
  0.0 453.9 jit_solution(17660821486023258840)
XLA Ops:
  8.1 3.9 collective-permute-start
  12.0 1.3 collective-permute-start.1
  16.3 1.1 pad_maximum_fusion.8
  17.6 3.2 collective-permute-start.2
  20.8 1.3 collective-permute-start.3
  22.2 2.1 collective-permute-done.2
  24.2 3.8 collective-permute-done.3
  29.2 3.5 collective-permute-start.4
  32.7 1.3 collective-permute-start.5
  34.0 3.0 collective-permute-done.5
  37.2 3.3 collective-permute-start.6
  40.5 1.3 collective-permute-start.7
  41.8 2.2 collective-permute-done.6
  44.0 5.0 %collective-permute-done.7 = f32[4,130,1]{2,1,0:T(8,128)S(1)} collective-permute-done((f32[4,130,1]{2,1,0:T(8,128)S(1)}, f32[4,130,1]{2,1,0:T(8,128)S(1)}, u32[]{:S(2)}, u32[]{:S(2)}) %collective-permute-start.7) | collective-permute-done | bytes 2112 | tf_op jit(solution)/shard_map/ppermute | solution.py:30
  50.0 3.4 collective-permute-start.8
  53.4 1.3 collective-permute-start.9
  54.7 3.1 collective-permute-done.9
  58.0 4.6 %collective-permute-start.10 = (f32[4,130,1]{2,1,0:T(8,128)S(1)}, f32[4,130,1]{2,1,0:T(8,128)S(1)}, u32[]{:S(2)}, u32[]{:S(2)}) collective-permute-start(f32[4,130,1]{2,1,0:T(8,128)S(1)} %get-tuple-element.37), channel_id=1, source_target_pairs={{0,16},{16,32},{32,48},{48,64},{64,80},{80,96},{96,112},{1,17},{17... | collective-permute-start | bytes 6248 | tf_op jit(solution)/shard_map/ppermute | solution.py:28
  62.6 1.3 collective-permute-start.11
  63.9 2.2 collective-permute-done.10
  66.0 3.8 collective-permute-done.11
  71.0 3.4 collective-permute-start.12
  74.3 1.3 collective-permute-start.13
  75.6 3.0 collective-permute-done.13
  78.9 3.4 collective-permute-start.14
  82.2 1.3 collective-permute-start.15
  83.5 2.2 collective-permute-done.14
  85.7 3.8 collective-permute-done.15
  90.6 2.2 collective-permute-start.16
  92.9 1.3 collective-permute-start.17
  94.2 3.3 collective-permute-done.17
  97.7 2.8 collective-permute-start.18
  100.5 1.3 collective-permute-start.19
  101.8 2.2 collective-permute-done.18
  104.0 3.8 collective-permute-done.19
  108.9 2.1 collective-permute-start.20
  111.1 1.3 collective-permute-start.21
  112.4 3.0 collective-permute-done.21
  115.6 3.2 collective-permute-start.22
  118.8 1.3 collective-permute-start.23
  120.1 2.2 collective-permute-done.22
  122.3 3.8 collective-permute-done.23
  127.2 2.2 collective-permute-start.24
  129.4 1.3 collective-permute-start.25
  130.8 3.0 collective-permute-done.25
  134.0 2.9 collective-permute-start.26
  136.9 1.3 collective-permute-start.27
  138.2 2.1 collective-permute-done.26
  140.3 3.9 collective-permute-done.27
  145.3 1.3 collective-permute-start.29
  146.6 4.2 collective-permute-start.28
  151.5 1.3 collective-permute-start.31
  152.8 4.0 collective-permute-start.30
  156.9 3.6 collective-permute-done.31
  160.5 1.9 negate_multiply_fusion
  163.5 142.6 %all-reduce.3.cloned.1.call-done = f32[4,128,256]{2,1,0:T(8,128)} async-done(((f32[4,128,256]{2,1,0:T(8,128)}), f32[4,128,256]{2,1,0:T(8,128)}) %all-reduce.3.cloned.1.call-update) | async-done | bytes 524304 | tf_op jit(solution)/shard_map/pmax | solution.py:102
  306.1 2.3 select_reduce_fusion
  308.8 117.1 %all-reduce.5.cloned.1.call-done = f32[4,128,256]{2,1,0:T(8,128)} async-done(((f32[4,128,256]{2,1,0:T(8,128)}), f32[4,128,256]{2,1,0:T(8,128)}) %all-reduce.5.cloned.1.call-update) | async-done | bytes 524304 | tf_op jit(solution)/shard_map/psum | solution.py:104
  425.8 1.1 add_multiply_fusion
  427.0 1.3 collective-permute-start.33
  428.3 4.0 collective-permute-start.32
  433.8 1.3 collective-permute-start.35
  435.5 4.0 collective-permute-start.34
  443.9 1.1 copy.38
  (97 shorter events, 23.3 us)
Async XLA Ops:
  7.2 20.9 %copy-start.1 = (f32[4,128,256]{2,1,0:T(8,128)S(1)}, f32[4,128,256]{2,1,0:T(8,128)}, u32[]{:S(2)}) copy-start(f32[4,128,256]{2,1,0:T(8,128)} %param.6) | copy-start | bytes 1572868
  7.2 298.9 %all-reduce.3.cloned.1.call-start = ((), (), s32[]{:S(2)}) async-start(), calls=%async_computation | async-start | bytes 1048576 | tf_op jit(solution)/shard_map/pmax | solution.py:102
  8.1 7.3 %collective-permute-start = (f32[4,1,256]{2,1,0:T(1,128)S(1)}, f32[4,1,256]{2,1,0:T(1,128)S(1)}, u32[]{:S(2)}, u32[]{:S(2)}) collective-permute-start(f32[4,1,256]{2,1,0:T(1,128)S(1)} %get-tuple-element.57), channel_id=1, source_target_pairs={{0,128},{128,256},{256,384},{1,129},{129,257},{257,385},{2,130},{1... | collective-permute-start | bytes 12296 | tf_op jit(solution)/shard_map/ppermute | solution.py:28
  12.0 4.4 collective-permute-start.1
  17.6 6.7 %collective-permute-start.2 = (f32[4,130,1]{2,1,0:T(8,128)S(1)}, f32[4,130,1]{2,1,0:T(8,128)S(1)}, u32[]{:S(2)}, u32[]{:S(2)}) collective-permute-start(f32[4,130,1]{2,1,0:T(8,128)S(1)} %get-tuple-element.41), channel_id=1, source_target_pairs={{0,16},{16,32},{32,48},{48,64},{64,80},{80,96},{96,112},{1,17},{17... | collective-permute-start | bytes 6248 | tf_op jit(solution)/shard_map/ppermute | solution.py:28
  20.8 7.3 %collective-permute-start.3 = (f32[4,130,1]{2,1,0:T(8,128)S(1)}, f32[4,130,1]{2,1,0:T(8,128)S(1)}, u32[]{:S(2)}, u32[]{:S(2)}) collective-permute-start(f32[4,130,1]{2,1,0:T(8,128)S(1)} %get-tuple-element.40), channel_id=1, source_target_pairs={{16,0},{32,16},{48,32},{64,48},{80,64},{96,80},{112,96},{17,1},{33... | collective-permute-start | bytes 6248 | tf_op jit(solution)/shard_map/ppermute | solution.py:30
  29.2 4.8 %collective-permute-start.4 = (f32[4,1,256]{2,1,0:T(1,128)S(1)}, f32[4,1,256]{2,1,0:T(1,128)S(1)}, u32[]{:S(2)}, u32[]{:S(2)}) collective-permute-start(f32[4,1,256]{2,1,0:T(1,128)S(1)} %get-tuple-element.55), channel_id=1, source_target_pairs={{0,128},{128,256},{256,384},{1,129},{129,257},{257,385},{2,130},{1... | collective-permute-start | bytes 12296 | tf_op jit(solution)/shard_map/ppermute | solution.py:28
  32.7 4.4 collective-permute-start.5
  37.2 6.8 %collective-permute-start.6 = (f32[4,130,1]{2,1,0:T(8,128)S(1)}, f32[4,130,1]{2,1,0:T(8,128)S(1)}, u32[]{:S(2)}, u32[]{:S(2)}) collective-permute-start(f32[4,130,1]{2,1,0:T(8,128)S(1)} %get-tuple-element.39), channel_id=1, source_target_pairs={{0,16},{16,32},{32,48},{48,64},{64,80},{80,96},{96,112},{1,17},{17... | collective-permute-start | bytes 6248 | tf_op jit(solution)/shard_map/ppermute | solution.py:28
  40.5 8.5 %collective-permute-start.7 = (f32[4,130,1]{2,1,0:T(8,128)S(1)}, f32[4,130,1]{2,1,0:T(8,128)S(1)}, u32[]{:S(2)}, u32[]{:S(2)}) collective-permute-start(f32[4,130,1]{2,1,0:T(8,128)S(1)} %get-tuple-element.38), channel_id=1, source_target_pairs={{16,0},{32,16},{48,32},{64,48},{80,64},{96,80},{112,96},{17,1},{33... | collective-permute-start | bytes 6248 | tf_op jit(solution)/shard_map/ppermute | solution.py:30
  50.0 4.7 %collective-permute-start.8 = (f32[4,1,256]{2,1,0:T(1,128)S(1)}, f32[4,1,256]{2,1,0:T(1,128)S(1)}, u32[]{:S(2)}, u32[]{:S(2)}) collective-permute-start(f32[4,1,256]{2,1,0:T(1,128)S(1)} %get-tuple-element.53), channel_id=1, source_target_pairs={{0,128},{128,256},{256,384},{1,129},{129,257},{257,385},{2,130},{1... | collective-permute-start | bytes 12296 | tf_op jit(solution)/shard_map/ppermute | solution.py:28
  53.4 4.4 collective-permute-start.9
  58.0 8.0 %collective-permute-start.10 = (f32[4,130,1]{2,1,0:T(8,128)S(1)}, f32[4,130,1]{2,1,0:T(8,128)S(1)}, u32[]{:S(2)}, u32[]{:S(2)}) collective-permute-start(f32[4,130,1]{2,1,0:T(8,128)S(1)} %get-tuple-element.37), channel_id=1, source_target_pairs={{0,16},{16,32},{32,48},{48,64},{64,80},{80,96},{96,112},{1,17},{17... | collective-permute-start | bytes 6248 | tf_op jit(solution)/shard_map/ppermute | solution.py:28
  62.6 7.3 %collective-permute-start.11 = (f32[4,130,1]{2,1,0:T(8,128)S(1)}, f32[4,130,1]{2,1,0:T(8,128)S(1)}, u32[]{:S(2)}, u32[]{:S(2)}) collective-permute-start(f32[4,130,1]{2,1,0:T(8,128)S(1)} %get-tuple-element.36), channel_id=1, source_target_pairs={{16,0},{32,16},{48,32},{64,48},{80,64},{96,80},{112,96},{17,1},{33... | collective-permute-start | bytes 6248 | tf_op jit(solution)/shard_map/ppermute | solution.py:30
  71.0 4.7 %collective-permute-start.12 = (f32[4,1,256]{2,1,0:T(1,128)S(1)}, f32[4,1,256]{2,1,0:T(1,128)S(1)}, u32[]{:S(2)}, u32[]{:S(2)}) collective-permute-start(f32[4,1,256]{2,1,0:T(1,128)S(1)} %get-tuple-element.51), channel_id=1, source_target_pairs={{0,128},{128,256},{256,384},{1,129},{129,257},{257,385},{2,130},{1... | collective-permute-start | bytes 12296 | tf_op jit(solution)/shard_map/ppermute | solution.py:28
  74.3 4.4 collective-permute-start.13
  78.9 6.8 %collective-permute-start.14 = (f32[4,130,1]{2,1,0:T(8,128)S(1)}, f32[4,130,1]{2,1,0:T(8,128)S(1)}, u32[]{:S(2)}, u32[]{:S(2)}) collective-permute-start(f32[4,130,1]{2,1,0:T(8,128)S(1)} %get-tuple-element.35), channel_id=1, source_target_pairs={{0,16},{16,32},{32,48},{48,64},{64,80},{80,96},{96,112},{1,17},{17... | collective-permute-start | bytes 6248 | tf_op jit(solution)/shard_map/ppermute | solution.py:28
  82.2 7.3 %collective-permute-start.15 = (f32[4,130,1]{2,1,0:T(8,128)S(1)}, f32[4,130,1]{2,1,0:T(8,128)S(1)}, u32[]{:S(2)}, u32[]{:S(2)}) collective-permute-start(f32[4,130,1]{2,1,0:T(8,128)S(1)} %get-tuple-element.34), channel_id=1, source_target_pairs={{16,0},{32,16},{48,32},{64,48},{80,64},{96,80},{112,96},{17,1},{33... | collective-permute-start | bytes 6248 | tf_op jit(solution)/shard_map/ppermute | solution.py:30
  90.6 3.5 collective-permute-start.16
  92.9 4.6 %collective-permute-start.17 = (f32[4,1,256]{2,1,0:T(1,128)S(1)}, f32[4,1,256]{2,1,0:T(1,128)S(1)}, u32[]{:S(2)}, u32[]{:S(2)}) collective-permute-start(f32[4,1,256]{2,1,0:T(1,128)S(1)} %get-tuple-element.48), channel_id=1, source_target_pairs={{128,0},{256,128},{384,256},{129,1},{257,129},{385,257},{130,2},{2... | collective-permute-start | bytes 12296 | tf_op jit(solution)/shard_map/ppermute | solution.py:30
  97.7 6.3 %collective-permute-start.18 = (f32[4,130,1]{2,1,0:T(8,128)S(1)}, f32[4,130,1]{2,1,0:T(8,128)S(1)}, u32[]{:S(2)}, u32[]{:S(2)}) collective-permute-start(f32[4,130,1]{2,1,0:T(8,128)S(1)} %get-tuple-element.33), channel_id=1, source_target_pairs={{0,16},{16,32},{32,48},{48,64},{64,80},{80,96},{96,112},{1,17},{17... | collective-permute-start | bytes 6248 | tf_op jit(solution)/shard_map/ppermute | solution.py:28
  100.5 7.3 %collective-permute-start.19 = (f32[4,130,1]{2,1,0:T(8,128)S(1)}, f32[4,130,1]{2,1,0:T(8,128)S(1)}, u32[]{:S(2)}, u32[]{:S(2)}) collective-permute-start(f32[4,130,1]{2,1,0:T(8,128)S(1)} %get-tuple-element.32), channel_id=1, source_target_pairs={{16,0},{32,16},{48,32},{64,48},{80,64},{96,80},{112,96},{17,1},{33... | collective-permute-start | bytes 6248 | tf_op jit(solution)/shard_map/ppermute | solution.py:30
  108.9 3.4 collective-permute-start.20
  111.1 4.4 collective-permute-start.21
  115.6 6.7 %collective-permute-start.22 = (f32[4,130,1]{2,1,0:T(8,128)S(1)}, f32[4,130,1]{2,1,0:T(8,128)S(1)}, u32[]{:S(2)}, u32[]{:S(2)}) collective-permute-start(f32[4,130,1]{2,1,0:T(8,128)S(1)} %get-tuple-element.31), channel_id=1, source_target_pairs={{0,16},{16,32},{32,48},{48,64},{64,80},{80,96},{96,112},{1,17},{17... | collective-permute-start | bytes 6248 | tf_op jit(solution)/shard_map/ppermute | solution.py:28
  118.8 7.3 %collective-permute-start.23 = (f32[4,130,1]{2,1,0:T(8,128)S(1)}, f32[4,130,1]{2,1,0:T(8,128)S(1)}, u32[]{:S(2)}, u32[]{:S(2)}) collective-permute-start(f32[4,130,1]{2,1,0:T(8,128)S(1)} %get-tuple-element.30), channel_id=1, source_target_pairs={{16,0},{32,16},{48,32},{64,48},{80,64},{96,80},{112,96},{17,1},{33... | collective-permute-start | bytes 6248 | tf_op jit(solution)/shard_map/ppermute | solution.py:30
  127.2 3.5 collective-permute-start.24
  129.4 4.4 collective-permute-start.25
  134.0 6.3 %collective-permute-start.26 = (f32[4,130,1]{2,1,0:T(8,128)S(1)}, f32[4,130,1]{2,1,0:T(8,128)S(1)}, u32[]{:S(2)}, u32[]{:S(2)}) collective-permute-start(f32[4,130,1]{2,1,0:T(8,128)S(1)} %get-tuple-element.29), channel_id=1, source_target_pairs={{0,16},{16,32},{32,48},{48,64},{64,80},{80,96},{96,112},{1,17},{17... | collective-permute-start | bytes 6248 | tf_op jit(solution)/shard_map/ppermute | solution.py:28
  136.9 20.0 %copy-start.3 = (s32[4]{0:T(128)S(1)}, s32[4]{0:T(128)}, u32[]{:S(2)}) copy-start(s32[4]{0:T(128)} %param.11) | copy-start | bytes 52
  136.9 7.3 %collective-permute-start.27 = (f32[4,130,1]{2,1,0:T(8,128)S(1)}, f32[4,130,1]{2,1,0:T(8,128)S(1)}, u32[]{:S(2)}, u32[]{:S(2)}) collective-permute-start(f32[4,130,1]{2,1,0:T(8,128)S(1)} %get-tuple-element.28), channel_id=1, source_target_pairs={{16,0},{32,16},{48,32},{64,48},{80,64},{96,80},{112,96},{17,1},{33... | collective-permute-start | bytes 6248 | tf_op jit(solution)/shard_map/ppermute | solution.py:30
  145.3 5.5 %collective-permute-start.29 = (f32[4,1,256]{2,1,0:T(1,128)S(1)}, f32[4,1,256]{2,1,0:T(1,128)S(1)}, u32[]{:S(2)}, u32[]{:S(2)}) collective-permute-start(f32[4,1,256]{2,1,0:T(1,128)S(1)} %get-tuple-element.43), channel_id=1, source_target_pairs={{128,0},{256,128},{384,256},{129,1},{257,129},{385,257},{130,2},{2... | collective-permute-start | bytes 12296 | tf_op jit(solution)/shard_map/ppermute | solution.py:30
  146.6 4.7 %collective-permute-start.28 = (f32[4,1,256]{2,1,0:T(1,128)S(1)}, f32[4,1,256]{2,1,0:T(1,128)S(1)}, u32[]{:S(2)}, u32[]{:S(2)}) collective-permute-start(f32[4,1,256]{2,1,0:T(1,128)S(1)} %get-tuple-element.42), channel_id=1, source_target_pairs={{0,128},{128,256},{256,384},{1,129},{129,257},{257,385},{2,130},{1... | collective-permute-start | bytes 12296 | tf_op jit(solution)/shard_map/ppermute | solution.py:28
  151.5 9.0 %collective-permute-start.31 = (f32[4,130,1]{2,1,0:T(8,128)S(1)}, f32[4,130,1]{2,1,0:T(8,128)S(1)}, u32[]{:S(2)}, u32[]{:S(2)}) collective-permute-start(f32[4,130,1]{2,1,0:T(8,128)S(1)} %get-tuple-element.27), channel_id=1, source_target_pairs={{16,0},{32,16},{48,32},{64,48},{80,64},{96,80},{112,96},{17,1},{33... | collective-permute-start | bytes 6248 | tf_op jit(solution)/shard_map/ppermute | solution.py:30
  152.8 7.7 %collective-permute-start.30 = (f32[4,130,1]{2,1,0:T(8,128)S(1)}, f32[4,130,1]{2,1,0:T(8,128)S(1)}, u32[]{:S(2)}, u32[]{:S(2)}) collective-permute-start(f32[4,130,1]{2,1,0:T(8,128)S(1)} %get-tuple-element.26), channel_id=1, source_target_pairs={{0,16},{16,32},{32,48},{48,64},{64,80},{80,96},{96,112},{1,17},{17... | collective-permute-start | bytes 6248 | tf_op jit(solution)/shard_map/ppermute | solution.py:28
  163.4 262.4 %all-reduce.5.cloned.1.call-start = ((), (), s32[]{:S(2)}) async-start(), calls=%async_computation.1 | async-start | bytes 1048576 | tf_op jit(solution)/shard_map/psum | solution.py:104
  306.1 119.7 %copy-start.2 = (f32[4,128,256]{2,1,0:T(8,128)S(1)}, f32[4,128,256]{2,1,0:T(8,128)}, u32[]{:S(2)}) copy-start(f32[4,128,256]{2,1,0:T(8,128)} %all-reduce.3.cloned.1.call-done) | copy-start | bytes 1572868
  308.4 118.6 %copy-start = (f32[4,128,256]{2,1,0:T(8,128)S(1)}, f32[4,128,256]{2,1,0:T(8,128)}, u32[]{:S(2)}) copy-start(f32[4,128,256]{2,1,0:T(8,128)} %param.9) | copy-start | bytes 1572868
  427.0 5.5 %collective-permute-start.33 = (f32[8,2,256]{2,0,1:T(8,128)S(1)}, f32[8,2,256]{2,0,1:T(8,128)S(1)}, u32[]{:S(2)}, u32[]{:S(2)}) collective-permute-start(f32[8,2,256]{2,0,1:T(8,128)S(1)} %copy.27), channel_id=1, source_target_pairs={{128,0},{256,128},{384,256},{129,1},{257,129},{385,257},{130,2},{2... | collective-permute-start | bytes 49160 | tf_op jit(solution)/shard_map/ppermute | solution.py:30
  428.3 4.8 %collective-permute-start.32 = (f32[8,2,256]{2,0,1:T(8,128)S(1)}, f32[8,2,256]{2,0,1:T(8,128)S(1)}, u32[]{:S(2)}, u32[]{:S(2)}) collective-permute-start(f32[8,2,256]{2,0,1:T(8,128)S(1)} %copy.26), channel_id=1, source_target_pairs={{0,128},{128,256},{256,384},{1,129},{129,257},{257,385},{2,130},{1... | collective-permute-start | bytes 49160 | tf_op jit(solution)/shard_map/ppermute | solution.py:28
  433.8 5.8 %collective-permute-start.35 = (f32[8,132,2]{1,0,2:T(8,128)S(1)}, f32[8,132,2]{1,0,2:T(8,128)S(1)}, u32[]{:S(2)}, u32[]{:S(2)}) collective-permute-start(f32[8,132,2]{1,0,2:T(8,128)S(1)} %copy.31), channel_id=1, source_target_pairs={{16,0},{32,16},{48,32},{64,48},{80,64},{96,80},{112,96},{17,1},{33... | collective-permute-start | bytes 25352 | tf_op jit(solution)/shard_map/ppermute | solution.py:30
  435.5 4.8 %collective-permute-start.34 = (f32[8,132,2]{1,0,2:T(8,128)S(1)}, f32[8,132,2]{1,0,2:T(8,128)S(1)}, u32[]{:S(2)}, u32[]{:S(2)}) collective-permute-start(f32[8,132,2]{1,0,2:T(8,128)S(1)} %copy.30), channel_id=1, source_target_pairs={{0,16},{16,32},{32,48},{48,64},{64,80},{80,96},{96,112},{1,17},{17... | collective-permute-start | bytes 25352 | tf_op jit(solution)/shard_map/ppermute | solution.py:28
Sparse Core Ops, SparseCore 0:
  163.5 142.5 all-reduce.2
  309.0 116.7 all-reduce.4
where the time goes:
time: 459 us; the launch traced here: 454 us
  waiting for transfers between devices  328 us (71%)
  starting transfers between devices  83.5 us (18%)
  other arithmetic  22.8 us (5%)
  between operations  14.8 us (3%)
  local copies, waits for them, and re-layouts  5.24 us (1%)
    pmax x1, waiting for transfers between devices, goal_soft_min(): peak_score = lax.pmax(peak_score, 'goal')  143 us
    psum x1, waiting for transfers between devices, goal_soft_min(): weight_sum = lax.psum(local_sum, 'goal')  117 us
    ppermute x18, starting transfers between devices, extended_2(): lax.ppermute(tail, axis, [(i, (i + 1) % count) for i in range(ends)])  60.1 us
    ppermute x18, waiting for transfers between devices, extended_2(): lax.ppermute(head, axis, [((i + 1) % count, i) for i in range(ends)])  51.2 us
    ppermute x18, starting transfers between devices, extended_2(): lax.ppermute(head, axis, [((i + 1) % count, i) for i in range(ends)])  23.3 us
    ppermute x18, waiting for transfers between devices, extended_2(): lax.ppermute(tail, axis, [(i, (i + 1) % count) for i in range(ends)])  16.7 us
  transfers between devices with their start and end apart: 38, of which 27 were waited for; matrix products, arithmetic and copies ran while one was open for 1% of the time, Pallas kernels for 0%

commit v1 on v0

v1 whole, which is shorter than its diff:
```python
import functools

import jax
import jax.numpy as jnp
import numpy as np
from jax import lax
from jax.experimental import pallas as pl
from jax.experimental.pallas import tpu as pltpu
from jax.sharding import PartitionSpec as P

MESH = pl.DeviceIdType.MESH
SWEEPS = 8
CELL_SIZE = 0.005
SWEEP_TEMP = 0.002
GOAL_TEMP = 0.01
OBSTACLE_COST = 8.0
COURANT = 0.4
FAR = 10000.0
SHUT = 1e30
ABSENT = 1e28

LANES = 128
PAD = 16
K_SWEEP = float(1.0 / (SWEEP_TEMP * np.log(2.0)))
K_GOAL = float(1.0 / (GOAL_TEMP * np.log(2.0)))


def roll(x, shift):
    shift %= LANES
    return x if shift == 0 else pltpu.roll(x, shift, 1)


def soft_min(items, k, temp):
    least = functools.reduce(jnp.minimum, items)
    total = functools.reduce(jnp.add, [jnp.exp2((least - item) * k) for item in items])
    return least - temp * jnp.log(total)


def loop(start, stop, body, unroll=1):
    def step(i, carry):
        body(i)
        return carry

    lax.fori_loop(start, stop, step, 0, unroll=unroll)


def tile_at(row):
    return pl.ds(pl.multiple_of(row, 8), 8)


def kernel(
    nx, ny, nz, goals, groups, height, width,
    pot, cost, obst, dens, dest, gid,
    pot_out, vel_out, den_out,
    X, St, S, Ss, Cb, Ob, D, Ds, ML, MR, RL, RR,
    G, G2, H, R, F, Fs, FML, FMR, FRL, FRR, Vx, Vy, Vxs, Vys, DO,
    lsem, ssem, rsem,
):
    halves = width // LANES
    rows_all = height + 2 * PAD
    bottom = PAD + height
    chunk = height // nz
    ix, iy, ig = lax.axis_index("gx"), lax.axis_index("gy"), lax.axis_index("goal")
    z, core = ig // 2, ig % 2
    xs = {-1: lax.rem(ix + nx - 1, nx), 0: ix, 1: lax.rem(ix + 1, nx)}
    ys = {-1: lax.rem(iy + ny - 1, ny), 0: iy, 1: lax.rem(iy + 1, ny)}
    partner = (ix, iy, 2 * z + (1 - core))
    z_at = [lax.rem(z + d, nz) for d in range(nz)]
    z_back = [lax.rem(z + nz - d, nz) for d in range(nz)]
    z_peer = [(ix, iy, 2 * z_at[d] + core) for d in range(nz)]
    around = [(dx, dy) for dx in (-1, 0, 1) for dy in (-1, 0, 1) if (dx, dy) != (0, 0)]
    at_top, at_bottom = ix == 0, ix == nx - 1
    at_left, at_right = iy == 0, iy == ny - 1

    barrier = pltpu.get_barrier_semaphore()
    greet = [(xs[dx], ys[dy], ig) for dx, dy in around] + [partner] + z_peer[1:]
    for device in greet:
        pl.semaphore_signal(barrier, inc=1, device_id=device, device_id_type=MESH)

    count = [0]

    def local(src, dst):
        copy = pltpu.make_async_copy(src, dst, lsem.at[count[0]])
        count[0] += 1
        copy.start()
        return copy

    body_rows = pl.ds(PAD, height)
    first, last = pl.ds(0, 8), pl.ds(height - 8, 8)
    above, below = pl.ds(PAD - 8, 8), pl.ds(bottom, 8)
    p_first, p_last = pl.ds(PAD, 8), pl.ds(bottom - 8, 8)
    cut = [pl.ds(LANES * h, LANES) for h in range(halves)]

    cost_in = [local(cost.at[:, cut[h]], Cb.at[h]) for h in range(halves)]
    cost_in += [local(obst.at[:, cut[h]], Ob.at[h]) for h in range(halves)]
    field_in = [local(pot.at[:, :, cut[h]], X.at[0, :, h, body_rows]) for h in range(halves)]
    field_in += [local(dens.at[:, :, cut[h]], D.at[:, h, body_rows]) for h in range(halves)]

    sent = [0]

    def remote(src, dst, device):
        copy = pltpu.make_async_remote_copy(
            src_ref=src, dst_ref=dst, send_sem=ssem.at[sent[0]], recv_sem=rsem.at[sent[0]],
            device_id=device, device_id_type=MESH,
        )
        sent[0] += 1
        copy.start()
        return copy

    pl.semaphore_wait(barrier, len(greet))
    north, south = (xs[-1], ys[0], ig), (xs[1], ys[0], ig)
    halo = []
    for h in range(halves):
        halo.append(remote(pot.at[:, first, cut[h]], X.at[0, :, h, below], north))
        halo.append(remote(pot.at[:, last, cut[h]], X.at[0, :, h, above], south))
        halo.append(remote(dens.at[:, first, cut[h]], D.at[:, h, below], north))
        halo.append(remote(dens.at[:, last, cut[h]], D.at[:, h, above], south))

    lane = lax.broadcasted_iota(jnp.int32, (8, LANES), 1)
    sub = lax.broadcasted_iota(jnp.int32, (8, LANES), 0)
    slot = lane // 32
    offset = lane % 32

    for buffer in (0, 1):
        for h in range(halves):
            for g in range(goals):
                X[buffer, g, h, 0:8] = jnp.zeros((8, LANES), jnp.float32)
                X[buffer, g, h, rows_all - 8 : rows_all] = jnp.zeros((8, LANES), jnp.float32)
            St[buffer, h, 0:8] = jnp.zeros((8, LANES), jnp.float32)
            St[buffer, h, rows_all - 8 : rows_all] = jnp.zeros((8, LANES), jnp.float32)

    for copy in cost_in:
        copy.wait()

    def make_cost(i):
        for h in range(halves):
            blocked = Ob[h, tile_at(8 * i)].astype(jnp.float32)
            S[h, tile_at(PAD + 8 * i)] = (Cb[h, tile_at(8 * i)] + OBSTACLE_COST * blocked) * CELL_SIZE

    loop(0, height // 8, make_cost, unroll=2)
    halo.append(remote(S.at[:, p_first], S.at[:, below], north))
    halo.append(remote(S.at[:, p_last], S.at[:, above], south))
    for copy in field_in:
        copy.wait()

    def in_slots(tiles, shift):
        out = roll(tiles[0], shift)
        for g in range(1, len(tiles)):
            out = jnp.where(slot == g, roll(tiles[g], shift + 32 * g), out)
        return out

    def repeated(tile, shift):
        out = jnp.where(offset < 8, roll(tile, shift), 0.0)
        return out

    right_edge = 8 - LANES

    def pack(i):
        t = tile_at(PAD + 8 * i)
        tm = tile_at(8 * i)
        p = [X[0, g, halves - 1, t] for g in range(goals)]
        s = [S[halves - 1, t]] * goals
        d = [D[k, halves - 1, t] for k in range(groups)]
        out = in_slots(p, right_edge)
        out = jnp.where(offset < 8, out, in_slots(s, right_edge + 8))
        MR[tm] = jnp.where(offset < 16, out, in_slots(d, right_edge + 16))
        p = [X[0, g, 0, t] for g in range(goals)]
        s = [S[0, t]] * goals
        d = [D[k, 0, t] for k in range(groups)]
        out = in_slots(p, 24)
        out = jnp.where(offset >= 24, out, in_slots(s, 16))
        ML[tm] = jnp.where(offset >= 16, out, in_slots(d, 8))

    loop(0, height // 8, pack, unroll=2)

    def send_columns(mr, ml, rl, rr):
        out = [
            remote(mr, rl.at[body_rows], (xs[0], ys[1], ig)),
            remote(ml, rr.at[body_rows], (xs[0], ys[-1], ig)),
            remote(mr.at[first], rl.at[below], (xs[-1], ys[1], ig)),
            remote(mr.at[last], rl.at[above], (xs[1], ys[1], ig)),
            remote(ml.at[first], rr.at[below], (xs[-1], ys[-1], ig)),
            remote(ml.at[last], rr.at[above], (xs[1], ys[-1], ig)),
        ]
        return out

    halo += send_columns(MR, ML, RL, RR)
    for copy in halo:
        copy.wait()

    n_ext = height // 8 + 2
    own_left, own_right = offset >= 8, offset < 24

    def build(i):
        t = tile_at(PAD - 8 + 8 * i)
        from_left, from_right = RL[t], RR[t]
        s = jnp.where(own_left, in_slots([S[0, t]] * goals, 8), roll(from_left, -8))
        s_left = jnp.where(at_left & ~own_left, SHUT, s)
        p = jnp.where(own_left, in_slots([X[0, g, 0, t] for g in range(goals)], 8), from_left)
        St[0, 0, t] = jnp.where(at_left & ~own_left, FAR - roll(s, -1), p)
        Ss[0, t] = s_left
        Ds[0, t] = jnp.where(
            own_left, in_slots([D[k, 0, t] for k in range(groups)], 8), roll(from_left, -16)
        )
        shift = 24 - LANES
        s = jnp.where(own_right, in_slots([S[halves - 1, t]] * goals, shift), roll(from_right, 8))
        s_right = jnp.where(at_right & ~own_right, SHUT, s)
        p = jnp.where(
            own_right, in_slots([X[0, g, halves - 1, t] for g in range(goals)], shift), from_right
        )
        St[0, 1, t] = jnp.where(at_right & ~own_right, FAR - roll(s, 1), p)
        Ss[1, t] = s_right
        Ds[1, t] = jnp.where(
            own_right, in_slots([D[k, halves - 1, t] for k in range(groups)], shift), roll(from_right, 16)
        )

    loop(0, n_ext, build)

    for flag, ghost, inner in ((at_top, above, PAD), (at_bottom, below, bottom - 1)):
        for h in range(halves):
            beside = jnp.broadcast_to(FAR - S[h, inner : inner + 1], (8, LANES))
            for g in range(goals):
                X[0, g, h, ghost] = jnp.where(flag, beside, X[0, g, h, ghost])
            S[h, ghost] = jnp.where(flag, SHUT, S[h, ghost])
        for side in (0, 1):
            beside = Ss[side, inner : inner + 1]
            beside = jnp.where(beside < SHUT, FAR - beside, FAR)
            beside = jnp.broadcast_to(beside, (8, LANES))
            St[0, side, ghost] = jnp.where(flag, beside, St[0, side, ghost])
            Ss[side, ghost] = jnp.where(flag, SHUT, Ss[side, ghost])

    width_all = width * ny
    cell = sub * width + lane
    target, strip_row = [], [jnp.full((8, LANES), -1000, jnp.int32) for _ in (0, 1)]
    for g in range(goals):
        row = dest[g] // width_all - ix * height
        col = dest[g] % width_all - iy * width
        held = (col >= 0) & (col < width)
        target.append(jnp.where(held, row * width + col, -(1 << 24)))
        for side, start in ((0, -8), (1, width - 24)):
            here = (slot == g) & (offset + start == col)
            strip_row[side] = jnp.where(here, row, strip_row[side])

    def relax(centre, up, down, left, right, s):
        return soft_min([centre, up + s, down + s, left + s, right + s], K_SWEEP, SWEEP_TEMP)

    def sweep(now, later, lo, hi):
        def tile(i):
            base = PAD - 8 + 8 * i
            t, tu, td = tile_at(base), pl.ds(base - 1, 8), pl.ds(base + 1, 8)
            row = 8 * i - 8
            s = [S[h, t] for h in range(halves)]
            for g in range(goals):
                centre = [X[now, g, h, t] for h in range(halves)]
                to_right = [roll(c, 1) for c in centre]
                to_left = [roll(c, -1) for c in centre]
                for h in range(halves):
                    left, right = to_right[h], to_left[h]
                    if h > 0:
                        left = jnp.where(lane == 0, to_right[h - 1], left)
                    if h < halves - 1:
                        right = jnp.where(lane == LANES - 1, to_left[h + 1], right)
                    new = relax(centre[h], X[now, g, h, tu], X[now, g, h, td], left, right, s[h])
                    pinned = cell == target[g] - (row * width + LANES * h)
                    X[later, g, h, t] = jnp.where(pinned, 0.0, new)
            for side in (0, 1):
                c = St[now, side, t]
                new = relax(c, St[now, side, tu], St[now, side, td], roll(c, 1), roll(c, -1), Ss[side, t])
                St[later, side, t] = jnp.where(strip_row[side] == sub + row, 0.0, new)

        loop(lo, hi, tile)

    def two_sweeps(j):
        sweep(0, 1, 0, n_ext)
        sweep(1, 0, 0, n_ext)

    loop(0, SWEEPS // 2, two_sweeps)

    bias = [[jnp.where(gid[g] == k, 0.0, ABSENT) for k in range(groups)] for g in range(goals)]

    def merged(main, left, right, g, h):
        if h == 0:
            main = jnp.where(lane < 8, roll(left, -(32 * g + 8)), main)
        if h == halves - 1:
            main = jnp.where(lane >= LANES - 8, roll(right, LANES - 24 - 32 * g), main)
        return main

    def finish(i):
        t = tile_at(PAD + 8 * i)
        strips = [St[0, side, t] for side in (0, 1)]
        for h in range(halves):
            p = [merged(X[0, g, h, t], strips[0], strips[1], g, h) for g in range(goals)]
            for g in range(goals):
                X[0, g, h, t] = p[g]
            for k in range(groups):
                G[k, h, tile_at(8 * i)] = soft_min(
                    [p[g] + bias[g][k] for g in range(goals)], K_GOAL, GOAL_TEMP
                )

    loop(0, height // 8, finish)
    outs = [local(X.at[0, :, h, body_rows], pot_out.at[:, :, cut[h]]) for h in range(halves)]

    swap = remote(G.at[:, 1 - core], G2, partner)
    swap.wait()

    def join(i):
        t = tile_at(8 * i)
        for k in range(groups):
            H[k, t] = soft_min([G[k, core, t], G2[k, t]], K_GOAL, GOAL_TEMP)

    loop(0, height // 8, join)

    def block(j):
        return pl.ds(pl.multiple_of(chunk * j, 8), chunk)

    def field_block(j):
        return pl.ds(pl.multiple_of(PAD + chunk * j, 8), chunk)

    order = sorted(range(1, nz), key=lambda d: -min(d, nz - d))
    spread = [remote(H.at[:, block(z_at[d])], R.at[d], z_peer[d]) for d in order]
    for copy in spread:
        copy.wait()
    for k in range(groups):
        for i in range(chunk // 8):
            t = slice(8 * i, 8 * i + 8)
            items = [H[k, tile_at(chunk * z + 8 * i)]] + [R[d, k, t] for d in range(1, nz)]
            F[k, core, tile_at(PAD + chunk * z + 8 * i)] = soft_min(items, K_GOAL, GOAL_TEMP)

    def mine(j):
        return F.at[:, core, field_block(j)]

    gather = {d: remote(mine(z), mine(z), z_peer[d]) for d in order}
    forward = [remote(mine(z), mine(z), partner)]
    for d in sorted(range(1, nz), key=lambda d: min(d, nz - d)):
        gather[d].wait_recv()
        forward.append(remote(mine(z_back[d]), mine(z_back[d]), partner))
    for d in order:
        gather[d].wait_send()
    for copy in forward:
        copy.wait()

    halo = [
        remote(F.at[:, :, p_first], F.at[:, :, below], north),
        remote(F.at[:, :, p_last], F.at[:, :, above], south),
    ]

    def pack_field(i):
        t = tile_at(PAD + 8 * i)
        FMR[tile_at(8 * i)] = in_slots([F[k, halves - 1, t] for k in range(groups)], right_edge)
        FML[tile_at(8 * i)] = in_slots([F[k, 0, t] for k in range(groups)], 24)

    loop(0, height // 8, pack_field, unroll=2)
    halo += send_columns(FMR, FML, FRL, FRR)
    for copy in halo:
        copy.wait()

    for flag, ghost, inner in ((at_top, above, PAD), (at_bottom, below, bottom - 1)):
        for h in range(halves):
            for k in range(groups):
                beside = jnp.broadcast_to(F[k, h, inner : inner + 1], (8, LANES))
                F[k, h, ghost] = jnp.where(flag, beside, F[k, h, ghost])

    def build_field(i):
        t = tile_at(PAD - 8 + 8 * i)
        f = jnp.where(own_left, in_slots([F[k, 0, t] for k in range(groups)], 8), FRL[t])
        Fs[0, t] = jnp.where(at_left & ~own_left, roll(f, -1), f)
        f = jnp.where(
            own_right, in_slots([F[k, halves - 1, t] for k in range(groups)], 24 - LANES), FRR[t]
        )
        Fs[1, t] = jnp.where(at_right & ~own_right, roll(f, 1), f)

    loop(0, n_ext, build_field)
    for flag, ghost, inner in ((at_top, above, PAD), (at_bottom, below, bottom - 1)):
        for side in (0, 1):
            beside = jnp.broadcast_to(Fs[side, inner : inner + 1], (8, LANES))
            Fs[side, ghost] = jnp.where(flag, beside, Fs[side, ghost])

    inv_two_cells = 1.0 / (2.0 * CELL_SIZE)

    def flow(up, down, left, right, speed):
        gx = (down - up) * inv_two_cells
        gy = (right - left) * inv_two_cells
        scale = speed * lax.rsqrt(1.0 + gx * gx + gy * gy)
        return -scale * gx, -scale * gy

    def sides(tiles, h):
        left, right = roll(tiles[h], 1), roll(tiles[h], -1)
        if h > 0:
            left = jnp.where(lane == 0, roll(tiles[h - 1], 1), left)
        if h < halves - 1:
            right = jnp.where(lane == LANES - 1, roll(tiles[h + 1], -1), right)
        return left, right

    def flows(i):
        base = PAD - 8 + 8 * i
        t, tu, td = tile_at(base), pl.ds(base - 1, 8), pl.ds(base + 1, 8)
        speed = []
        for h in range(halves):
            total = functools.reduce(jnp.add, [D[k, h, t] for k in range(groups)])
            speed.append(1.0 / (1.0 + total))
        for k in range(groups):
            centre = [F[k, h, t] for h in range(halves)]
            for h in range(halves):
                left, right = sides(centre, h)
                Vx[k, h, t], Vy[k, h, t] = flow(F[k, h, tu], F[k, h, td], left, right, speed[h])
        for side in (0, 1):
            d = Ds[side, t]
            d = d + roll(d, 32)
            d = d + roll(d, 64)
            c = Fs[side, t]
            Vxs[side, t], Vys[side, t] = flow(
                Fs[side, tu], Fs[side, td], roll(c, 1), roll(c, -1), 1.0 / (1.0 + d)
            )

    loop(0, n_ext, flows)

    def flux(low_v, high_v, low_d, high_d):
        face = 0.5 * (low_v + high_v)
        return jnp.maximum(face, 0.0) * low_d + jnp.minimum(face, 0.0) * high_d

    def advect(i):
        base = PAD + 8 * i
        t, tu, td = tile_at(base), pl.ds(base - 1, 8), pl.ds(base + 1, 8)
        row = sub + 8 * i
        no_up = at_top & (row == 0)
        no_down = at_bottom & (row == height - 1)

        def updated(vx, vxu, vxd, vy, vyl, vyr, d, du, dd, dl, dr, no_left, no_right):
            up = jnp.where(no_up, 0.0, flux(vxu, vx, du, d))
            down = jnp.where(no_down, 0.0, flux(vx, vxd, d, dd))
            left, right = flux(vyl, vy, dl, d), flux(vy, vyr, d, dr)
            left = left if no_left is None else jnp.where(no_left, 0.0, left)
            right = right if no_right is None else jnp.where(no_right, 0.0, right)
            return d - COURANT * (down - up + right - left)

        strips = []
        for side in (0, 1):
            vy, d = Vys[side, t], Ds[side, t]
            new = updated(
                Vxs[side, t], Vxs[side, tu], Vxs[side, td], vy, roll(vy, 1), roll(vy, -1),
                d, Ds[side, tu], Ds[side, td], roll(d, 1), roll(d, -1),
                (at_left & (offset == 8)) if side == 0 else None,
                (at_right & (offset == 23)) if side == 1 else None,
            )
            strips.append((Vxs[side, t], vy, new))
        for k in range(groups):
            vy = [Vy[k, h, t] for h in range(halves)]
            d = [D[k, h, t] for h in range(halves)]
            fresh = []
            for h in range(halves):
                vyl, vyr = sides(vy, h)
                dl, dr = sides(d, h)
                new = updated(
                    Vx[k, h, t], Vx[k, h, tu], Vx[k, h, td], vy[h], vyl, vyr,
                    d[h], D[k, h, tu], D[k, h, td], dl, dr, None, None,
                )
                fresh.append(new)
            for h in range(halves):
                DO[k, h, tile_at(8 * i)] = merged(fresh[h], strips[0][2], strips[1][2], k, h)

    loop(0, height // 8, advect)

    def merge_flow(i):
        t = tile_at(PAD + 8 * i)
        for k in range(groups):
            for h in range(halves):
                Vx[k, h, t] = merged(Vx[k, h, t], Vxs[0, t], Vxs[1, t], k, h)
                Vy[k, h, t] = merged(Vy[k, h, t], Vys[0, t], Vys[1, t], k, h)

    loop(0, height // 8, merge_flow)
    for h in range(halves):
        outs.append(local(Vx.at[:, h, body_rows], vel_out.at[:, 0, :, cut[h]]))
        outs.append(local(Vy.at[:, h, body_rows], vel_out.at[:, 1, :, cut[h]]))
        outs.append(local(DO.at[:, h], den_out.at[:, :, cut[h]]))
    for copy in outs:
        copy.wait()


def solution(mesh):
    nx, ny, ng = mesh.shape["gx"], mesh.shape["gy"], mesh.shape["goal"]

    def per_device(potential, cost, obstacle, density, destinations, group_ids):
        goals, height, width = potential.shape
        groups = density.shape[0]
        halves = width // LANES
        rows = height + 2 * PAD
        nz = ng // 2
        f32 = jnp.float32

        def vm(*shape, dtype=f32):
            return pltpu.VMEM(shape, dtype)

        panel = (rows, LANES)
        flat = (height, LANES)
        scratch = [
            vm(2, goals, halves, *panel), vm(2, 2, *panel), vm(halves, *panel), vm(2, *panel),
            vm(halves, *flat), vm(halves, *flat, dtype=jnp.int32),
            vm(groups, halves, *panel), vm(2, *panel), vm(*flat), vm(*flat), vm(*panel), vm(*panel),
            vm(groups, halves, *flat), vm(groups, *flat), vm(groups, *flat),
            vm(nz, groups, height // nz, LANES), vm(groups, halves, *panel), vm(2, *panel),
            vm(*flat), vm(*flat), vm(*panel), vm(*panel),
            vm(groups, halves, *panel), vm(groups, halves, *panel), vm(2, *panel), vm(2, *panel),
            vm(groups, halves, *flat),
            pltpu.SemaphoreType.DMA((24,)),
            pltpu.SemaphoreType.DMA((64,)),
            pltpu.SemaphoreType.DMA((64,)),
        ]
        anywhere = pl.BlockSpec(memory_space=pl.ANY)
        scalars = pl.BlockSpec(memory_space=pltpu.SMEM)
        return pl.pallas_call(
            functools.partial(kernel, nx, ny, nz, goals, groups, height, width),
            out_shape=(
                jax.ShapeDtypeStruct(potential.shape, f32),
                jax.ShapeDtypeStruct((groups, 2, height, width), f32),
                jax.ShapeDtypeStruct(density.shape, f32),
            ),
            in_specs=[anywhere] * 4 + [scalars] * 2,
            out_specs=(anywhere,) * 3,
            scratch_shapes=scratch,
            compiler_params=pltpu.CompilerParams(
                collective_id=0, has_side_effects=True, vmem_limit_bytes=40 << 20
            ),
            name="crowd_step",
        )(potential, cost, obstacle, density, destinations, group_ids)

    in_specs = (
        P("goal", "gx", "gy"),
        P("gx", "gy"),
        P("gx", "gy"),
        P(None, "gx", "gy"),
        P("goal"),
        P("goal"),
    )
    out_specs = (P("goal", "gx", "gy"), P(None, None, "gx", "gy"), P(None, "gx", "gy"))
    return jax.shard_map(
        per_device, mesh=mesh, in_specs=in_specs, out_specs=out_specs, check_vma=False
    )
```

time: 459 us -> 88.2 us (0.19); the launches traced: 454 us -> 87.9 us
  waiting for transfers between devices: 328 us -> 0 us
  starting transfers between devices: 83.5 us -> 0 us
  Pallas kernels: 0 us -> 79.5 us
  other arithmetic: 22.8 us -> 0 us
  between operations: 14.8 us -> 0.65 us
    pmax x1 -> x0, waiting for transfers between devices: 143 us -> none  [goal_soft_min(): peak_score = lax.pmax(peak_score, 'goal')]
    psum x1 -> x0, waiting for transfers between devices: 117 us -> none  [goal_soft_min(): weight_sum = lax.psum(local_sum, 'goal')]
    ppermute x36 -> x0, starting transfers between devices: 83.4 us -> none  [the longest x18 60.1 us: extended_2(): lax.ppermute(tail, axis, [(i, (i + 1) % count) for i in range(ends)])]
    pallas_call x0 -> x1, Pallas kernels: none -> 79.5 us  [per_device(): pl.pallas_call(functools.partial(kernel, nx, ny, nz, goals, groups, heigh...]
    ppermute x36 -> x0, waiting for transfers between devices: 67.8 us -> none  [the longest x18 51.2 us: extended_2(): lax.ppermute(head, axis, [((i + 1) % count, i) for i in range(ends)])]
    select_n x10 -> x0, other arithmetic: 9.18 us -> none  [the longest x7 7.55 us: relax_sweep(): return jnp.where(pinned, 0.0, lowest - SWEEP_TEMP * jnp.log(weight_sum))]
    unnamed x9 -> x15, local copies, waits for them, and re-layouts: 1.1 us -> 7.75 us
  transfers between devices with their start and end apart: 38 -> 0, of which waited for: 27 -> 0; matrix products, arithmetic and copies ran while one was open for 1% -> 0% of each run, Pallas kernels for 0% -> 0%
where the time goes in v1:
time: 88.2 us; the launch traced here: 87.9 us
  Pallas kernels  79.5 us (90%)
  local copies, waits for them, and re-layouts  7.75 us (9%)
    pallas_call x1, Pallas kernels, per_device(): pl.pallas_call(functools.partial(kernel, nx, ny, nz, goals, groups, heigh...  79.5 us
    unnamed x15, local copies, waits for them, and re-layouts  7.75 us

profile of v1, /device:TPU:1, one launch (start us, length us, event | category | flops | bytes accessed | tf_op | source)
XLA Modules:
  0.0 87.9 jit_solution(8098714227325735100)
XLA Ops:
  0.6 0.0 copy-start
  0.6 1.0 %copy-done = f32[4,128,256]{2,1,0:T(8,128)S(1)} copy-done((f32[4,128,256]{2,1,0:T(8,128)S(1)}, f32[4,128,256]{2,1,0:T(8,128)}, u32[]{:S(2)}) %copy-start) | copy-done | bytes 524312
  1.7 0.0 copy-start.1
  1.7 1.0 %copy-done.1 = f32[4,128,256]{2,1,0:T(8,128)S(1)} copy-done((f32[4,128,256]{2,1,0:T(8,128)S(1)}, f32[4,128,256]{2,1,0:T(8,128)}, u32[]{:S(2)}) %copy-start.1) | copy-done | bytes 524312
  2.7 0.0 copy-start.2
  2.7 0.9 %copy-done.2 = f32[128,256]{1,0:T(8,128)S(1)} copy-done((f32[128,256]{1,0:T(8,128)S(1)}, f32[128,256]{1,0:T(8,128)}, u32[]{:S(2)}) %copy-start.2) | copy-done | bytes 131096
  3.6 0.0 copy-start.3
  3.6 0.9 %copy-done.3 = s32[128,256]{1,0:T(8,128)S(1)} copy-done((s32[128,256]{1,0:T(8,128)S(1)}, s32[128,256]{1,0:T(8,128)}, u32[]{:S(2)}) %copy-start.3) | copy-done | bytes 131096
  4.5 0.0 copy-start.4
  4.5 0.7 copy-done.4
  5.2 0.0 copy-start.5
  5.2 0.7 copy-done.5
  5.8 79.5 %crowd_step.1 = (f32[4,128,256]{2,1,0:T(8,128)S(1)}, f32[4,2,128,256]{3,2,1,0:T(8,128)S(1)}, f32[4,128,256]{2,1,0:T(8,128)S(1)}) custom-call(f32[4,128,256]{2,1,0:T(8,128)S(1)} %copy-done, f32[128,256]{1,0:T(8,128)S(1)} %copy-done.2, s32[128,256]{1,0:T(8,128)S(1)} %copy-done.3, f32[4,128,256]{2,1,0:T(8,128)S(1)} %copy-done.1, s32[4]{0:T(128)S(1)} %copy-done.4, ...), custom_call_target="tpu_custom_call" | custom-call | tf_op jit(solution)/shard_map/crowd_step/pallas_call | solution.py:510
  85.4 0.8 copy.12
  86.2 1.0 %copy.13 = f32[4,2,128,256]{3,2,1,0:T(8,128)} copy(f32[4,2,128,256]{3,2,1,0:T(8,128)S(1)} %get-tuple-element.7) | data formatting | bytes 2097152
  87.1 0.8 copy.14
Async XLA Ops:
  0.6 1.0 %copy-start = (f32[4,128,256]{2,1,0:T(8,128)S(1)}, f32[4,128,256]{2,1,0:T(8,128)}, u32[]{:S(2)}) copy-start(f32[4,128,256]{2,1,0:T(8,128)} %pot.1) | copy-start | bytes 1572868
  1.7 1.0 %copy-start.1 = (f32[4,128,256]{2,1,0:T(8,128)S(1)}, f32[4,128,256]{2,1,0:T(8,128)}, u32[]{:S(2)}) copy-start(f32[4,128,256]{2,1,0:T(8,128)} %dens.1) | copy-start | bytes 1572868
  2.7 0.9 %copy-start.2 = (f32[128,256]{1,0:T(8,128)S(1)}, f32[128,256]{1,0:T(8,128)}, u32[]{:S(2)}) copy-start(f32[128,256]{1,0:T(8,128)} %cost.1) | copy-start | bytes 393220
  3.6 0.9 %copy-start.3 = (s32[128,256]{1,0:T(8,128)S(1)}, s32[128,256]{1,0:T(8,128)}, u32[]{:S(2)}) copy-start(s32[128,256]{1,0:T(8,128)} %obst.1) | copy-start | bytes 393220
  4.5 0.7 copy-start.4
  5.2 0.7 copy-start.5

commit v2 on v1

v2 whole, which is shorter than its diff:
```python
import functools

import jax
import jax.numpy as jnp
import numpy as np
from jax import lax
from jax.experimental import pallas as pl
from jax.experimental.pallas import tpu as pltpu
from jax.sharding import PartitionSpec as P

MESH = pl.DeviceIdType.MESH
SWEEPS = 8
CELL_SIZE = 0.005
SWEEP_TEMP = 0.002
GOAL_TEMP = 0.01
OBSTACLE_COST = 8.0
COURANT = 0.4
FAR = 10000.0
SHUT = 1e30
ABSENT = 1e28

LANES = 128
PAD = 16
U_SWEEP, U_BUILD, U_FIN = 9, 3, 4
K_SWEEP = float(1.0 / (SWEEP_TEMP * np.log(2.0)))
K_GOAL = float(1.0 / (GOAL_TEMP * np.log(2.0)))


def roll(x, shift):
    shift %= LANES
    return x if shift == 0 else pltpu.roll(x, shift, 1)


def soft_min(items, k, temp):
    least = functools.reduce(jnp.minimum, items)
    total = functools.reduce(jnp.add, [jnp.exp2((least - item) * k) for item in items])
    return least - temp * jnp.log(total)


def loop(start, stop, body, unroll=1):
    def step(i, carry):
        body(i)
        return carry

    lax.fori_loop(start, stop, step, 0, unroll=unroll)


def tile_at(row):
    return pl.ds(pl.multiple_of(row, 8), 8)


def kernel(
    nx, ny, nz, goals, groups, height, width,
    pot, cost, obst, dens, dest, gid,
    pot_out, vel_out, den_out,
    XA, XB, SA, SB, S, Ss, Cb, Ob, D, Ds, ML, MR, RL, RR,
    G, G2, H, R, F, Fs, FML, FMR, FRL, FRR, Vx, Vy, Vxs, Vys, DO,
    lsem, ssem, rsem,
):
    X, St = (XA, XB), (SA, SB)
    halves = width // LANES
    rows_all = height + 2 * PAD
    bottom = PAD + height
    ix, iy, ig = lax.axis_index("gx"), lax.axis_index("gy"), lax.axis_index("goal")
    z, core = ig // 2, ig % 2
    xs = {-1: lax.rem(ix + nx - 1, nx), 0: ix, 1: lax.rem(ix + 1, nx)}
    ys = {-1: lax.rem(iy + ny - 1, ny), 0: iy, 1: lax.rem(iy + 1, ny)}
    partner = (ix, iy, 2 * z + (1 - core))
    z_at = [lax.rem(z + d, nz) for d in range(nz)]
    z_back = [lax.rem(z + nz - d, nz) for d in range(nz)]
    z_peer = [(ix, iy, 2 * z_at[d] + core) for d in range(nz)]
    around = [(dx, dy) for dx in (-1, 0, 1) for dy in (-1, 0, 1) if (dx, dy) != (0, 0)]
    at_top, at_bottom = ix == 0, ix == nx - 1
    at_left, at_right = iy == 0, iy == ny - 1

    barrier = pltpu.get_barrier_semaphore()
    greet = [(xs[dx], ys[dy], ig) for dx, dy in around] + [partner] + z_peer[1:]
    for device in greet:
        pl.semaphore_signal(barrier, inc=1, device_id=device, device_id_type=MESH)

    count = [0]

    def local(src, dst):
        copy = pltpu.make_async_copy(src, dst, lsem.at[count[0]])
        count[0] += 1
        copy.start()
        return copy

    body_rows = pl.ds(PAD, height)
    first, last = pl.ds(0, 8), pl.ds(height - 8, 8)
    above, below = pl.ds(PAD - 8, 8), pl.ds(bottom, 8)
    p_first, p_last = pl.ds(PAD, 8), pl.ds(bottom - 8, 8)
    cut = [pl.ds(LANES * h, LANES) for h in range(halves)]

    cost_in = [local(cost.at[:, cut[h]], Cb.at[h]) for h in range(halves)]
    cost_in += [local(obst.at[:, cut[h]], Ob.at[h]) for h in range(halves)]
    field_in = [local(pot.at[:, :, cut[h]], XA.at[:, h, body_rows]) for h in range(halves)]
    field_in += [local(dens.at[:, :, cut[h]], D.at[:, h, body_rows]) for h in range(halves)]

    sent = [0]

    def remote(src, dst, device):
        copy = pltpu.make_async_remote_copy(
            src_ref=src, dst_ref=dst, send_sem=ssem.at[sent[0]], recv_sem=rsem.at[sent[0]],
            device_id=device, device_id_type=MESH,
        )
        sent[0] += 1
        copy.start()
        return copy

    pl.semaphore_wait(barrier, len(greet))
    north, south = (xs[-1], ys[0], ig), (xs[1], ys[0], ig)
    halo = []
    for h in range(halves):
        halo.append(remote(pot.at[:, first, cut[h]], XA.at[:, h, below], north))
        halo.append(remote(pot.at[:, last, cut[h]], XA.at[:, h, above], south))
        halo.append(remote(dens.at[:, first, cut[h]], D.at[:, h, below], north))
        halo.append(remote(dens.at[:, last, cut[h]], D.at[:, h, above], south))

    lane = lax.broadcasted_iota(jnp.int32, (8, LANES), 1)
    sub = lax.broadcasted_iota(jnp.int32, (8, LANES), 0)
    slot = lane // 32
    offset = lane % 32

    for buffer in (0, 1):
        for h in range(halves):
            for g in range(goals):
                X[buffer][g, h, 0:8] = jnp.zeros((8, LANES), jnp.float32)
                X[buffer][g, h, rows_all - 8 : rows_all] = jnp.zeros((8, LANES), jnp.float32)
            St[buffer][h, 0:8] = jnp.zeros((8, LANES), jnp.float32)
            St[buffer][h, rows_all - 8 : rows_all] = jnp.zeros((8, LANES), jnp.float32)

    for copy in cost_in:
        copy.wait()

    def make_cost(i):
        for h in range(halves):
            blocked = Ob[h, tile_at(8 * i)].astype(jnp.float32)
            S[h, tile_at(PAD + 8 * i)] = (Cb[h, tile_at(8 * i)] + OBSTACLE_COST * blocked) * CELL_SIZE

    loop(0, height // 8, make_cost, unroll=2)
    halo.append(remote(S.at[:, p_first], S.at[:, below], north))
    halo.append(remote(S.at[:, p_last], S.at[:, above], south))
    for copy in field_in:
        copy.wait()

    def in_slots(tiles, shift):
        out = roll(tiles[0], shift)
        for g in range(1, len(tiles)):
            out = jnp.where(slot == g, roll(tiles[g], shift + 32 * g), out)
        return out

    def repeated(tile, shift):
        out = jnp.where(offset < 8, roll(tile, shift), 0.0)
        return out

    right_edge = 8 - LANES

    def pack(i):
        t = tile_at(PAD + 8 * i)
        tm = tile_at(8 * i)
        p = [XA[g, halves - 1, t] for g in range(goals)]
        s = [S[halves - 1, t]] * goals
        d = [D[k, halves - 1, t] for k in range(groups)]
        out = in_slots(p, right_edge)
        out = jnp.where(offset < 8, out, in_slots(s, right_edge + 8))
        MR[tm] = jnp.where(offset < 16, out, in_slots(d, right_edge + 16))
        p = [XA[g, 0, t] for g in range(goals)]
        s = [S[0, t]] * goals
        d = [D[k, 0, t] for k in range(groups)]
        out = in_slots(p, 24)
        out = jnp.where(offset >= 24, out, in_slots(s, 16))
        ML[tm] = jnp.where(offset >= 16, out, in_slots(d, 8))

    loop(0, height // 8, pack, unroll=2)

    def send_columns(mr, ml, rl, rr):
        out = [
            remote(mr, rl.at[body_rows], (xs[0], ys[1], ig)),
            remote(ml, rr.at[body_rows], (xs[0], ys[-1], ig)),
            remote(mr.at[first], rl.at[below], (xs[-1], ys[1], ig)),
            remote(mr.at[last], rl.at[above], (xs[1], ys[1], ig)),
            remote(ml.at[first], rr.at[below], (xs[-1], ys[-1], ig)),
            remote(ml.at[last], rr.at[above], (xs[1], ys[-1], ig)),
        ]
        return out

    halo += send_columns(MR, ML, RL, RR)
    for copy in halo:
        copy.wait()

    n_ext = height // 8 + 2
    own_left, own_right = offset >= 8, offset < 24

    def build(i):
        t = tile_at(PAD - 8 + 8 * i)
        from_left, from_right = RL[t], RR[t]
        s = jnp.where(own_left, in_slots([S[0, t]] * goals, 8), roll(from_left, -8))
        s_left = jnp.where(at_left & ~own_left, SHUT, s)
        p = jnp.where(own_left, in_slots([XA[g, 0, t] for g in range(goals)], 8), from_left)
        SA[0, t] = jnp.where(at_left & ~own_left, FAR - roll(s, -1), p)
        Ss[0, t] = s_left
        Ds[0, t] = jnp.where(
            own_left, in_slots([D[k, 0, t] for k in range(groups)], 8), roll(from_left, -16)
        )
        shift = 24 - LANES
        s = jnp.where(own_right, in_slots([S[halves - 1, t]] * goals, shift), roll(from_right, 8))
        s_right = jnp.where(at_right & ~own_right, SHUT, s)
        p = jnp.where(
            own_right, in_slots([XA[g, halves - 1, t] for g in range(goals)], shift), from_right
        )
        SA[1, t] = jnp.where(at_right & ~own_right, FAR - roll(s, 1), p)
        Ss[1, t] = s_right
        Ds[1, t] = jnp.where(
            own_right, in_slots([D[k, halves - 1, t] for k in range(groups)], shift), roll(from_right, 16)
        )

    loop(0, n_ext, build, unroll=U_BUILD)

    for flag, ghost, inner in ((at_top, above, PAD), (at_bottom, below, bottom - 1)):
        for h in range(halves):
            beside = jnp.broadcast_to(FAR - S[h, inner : inner + 1], (8, LANES))
            for g in range(goals):
                XA[g, h, ghost] = jnp.where(flag, beside, XA[g, h, ghost])
            S[h, ghost] = jnp.where(flag, SHUT, S[h, ghost])
        for side in (0, 1):
            beside = Ss[side, inner : inner + 1]
            beside = jnp.where(beside < SHUT, FAR - beside, FAR)
            beside = jnp.broadcast_to(beside, (8, LANES))
            SA[side, ghost] = jnp.where(flag, beside, SA[side, ghost])
            Ss[side, ghost] = jnp.where(flag, SHUT, Ss[side, ghost])

    width_all = width * ny
    cell = sub * width + lane
    target, strip_row = [], [jnp.full((8, LANES), -1000, jnp.int32) for _ in (0, 1)]
    for g in range(goals):
        row = dest[g] // width_all - ix * height
        col = dest[g] % width_all - iy * width
        held = (col >= 0) & (col < width)
        target.append(jnp.where(held, row * width + col, -(1 << 24)))
        for side, start in ((0, -8), (1, width - 24)):
            here = (slot == g) & (offset + start == col)
            strip_row[side] = jnp.where(here, row, strip_row[side])

    def relax(centre, up, down, left, right, s):
        return soft_min([centre, up + s, down + s, left + s, right + s], K_SWEEP, SWEEP_TEMP)

    def sweep(now, later, lo, hi):
        def tile(i):
            base = PAD - 8 + 8 * i
            t, tu, td = tile_at(base), pl.ds(base - 1, 8), pl.ds(base + 1, 8)
            row = 8 * i - 8
            s = [S[h, t] for h in range(halves)]
            for g in range(goals):
                centre = [X[now][g, h, t] for h in range(halves)]
                to_right = [roll(c, 1) for c in centre]
                to_left = [roll(c, -1) for c in centre]
                for h in range(halves):
                    left, right = to_right[h], to_left[h]
                    if h > 0:
                        left = jnp.where(lane == 0, to_right[h - 1], left)
                    if h < halves - 1:
                        right = jnp.where(lane == LANES - 1, to_left[h + 1], right)
                    new = relax(centre[h], X[now][g, h, tu], X[now][g, h, td], left, right, s[h])
                    pinned = cell == target[g] - (row * width + LANES * h)
                    X[later][g, h, t] = jnp.where(pinned, 0.0, new)
            for side in (0, 1):
                c = St[now][side, t]
                new = relax(c, St[now][side, tu], St[now][side, td], roll(c, 1), roll(c, -1), Ss[side, t])
                St[later][side, t] = jnp.where(strip_row[side] == sub + row, 0.0, new)

        loop(lo, hi, tile, unroll=U_SWEEP)

    def two_sweeps(j):
        sweep(0, 1, 0, n_ext)
        sweep(1, 0, 0, n_ext)

    loop(0, SWEEPS // 2, two_sweeps)

    bias = [[jnp.where(gid[g] == k, 0.0, ABSENT) for k in range(groups)] for g in range(goals)]

    def merged(main, left, right, g, h):
        if h == 0:
            main = jnp.where(lane < 8, roll(left, -(32 * g + 8)), main)
        if h == halves - 1:
            main = jnp.where(lane >= LANES - 8, roll(right, LANES - 24 - 32 * g), main)
        return main

    def finish(i):
        t = tile_at(PAD + 8 * i)
        strips = [SA[side, t] for side in (0, 1)]
        for h in range(halves):
            p = [merged(XA[g, h, t], strips[0], strips[1], g, h) for g in range(goals)]
            for g in range(goals):
                XA[g, h, t] = p[g]
            for k in range(groups):
                G[k, h, tile_at(8 * i)] = soft_min(
                    [p[g] + bias[g][k] for g in range(goals)], K_GOAL, GOAL_TEMP
                )

    parts = 2
    part = height // parts
    tiles = part // 8
    outs, swap, spread, gather, forward = [], [], [], [], []

    def part_rows(q):
        return pl.ds(part * q, part)

    for q in range(parts):
        loop(tiles * q, tiles * (q + 1), finish, unroll=U_FIN)
        swap.append(remote(G.at[:, 1 - core, part_rows(q)], G2.at[:, part_rows(q)], partner))
    outs += [local(XA.at[:, h, body_rows], pot_out.at[:, :, cut[h]]) for h in range(halves)]

    def join(i):
        t = tile_at(8 * i)
        for k in range(groups):
            H[k, t] = soft_min([G[k, core, t], G2[k, t]], K_GOAL, GOAL_TEMP)

    chunk = part // nz

    def block(q, j):
        return pl.ds(pl.multiple_of(part * q + chunk * j, 8), chunk)

    order = sorted(range(1, nz), key=lambda d: -min(d, nz - d))
    for q in range(parts):
        swap[q].wait_recv()
        loop(tiles * q, tiles * (q + 1), join, unroll=2)
        spread.append([remote(H.at[:, block(q, z_at[d])], R.at[q, d], z_peer[d]) for d in order])

    def mine(q, j):
        return F.at[:, core, pl.ds(pl.multiple_of(PAD + part * q + chunk * j, 8), chunk)]

    for q in range(parts):
        for copy in spread[q]:
            copy.wait_recv()
        for k in range(groups):
            for i in range(chunk // 8):
                row = part * q + chunk * z + 8 * i
                items = [H[k, tile_at(row)]]
                items += [R[q, d, k, 8 * i : 8 * i + 8] for d in range(1, nz)]
                F[k, core, tile_at(PAD + row)] = soft_min(items, K_GOAL, GOAL_TEMP)
        gather.append({d: remote(mine(q, z), mine(q, z), z_peer[d]) for d in order})
        forward.append(remote(mine(q, z), mine(q, z), partner))

    def pack_field(i):
        t = tile_at(PAD + 8 * i)
        FMR[tile_at(8 * i)] = in_slots([F[k, halves - 1, t] for k in range(groups)], right_edge)
        FML[tile_at(8 * i)] = in_slots([F[k, 0, t] for k in range(groups)], 24)

    arrived = []
    for q in range(parts):
        for d in order[::-1]:
            gather[q][d].wait_recv()
            arrived.append(remote(mine(q, z_back[d]), mine(q, z_back[d]), partner))
    for q in range(parts):
        forward[q].wait_recv()
        for copy in arrived[q * (nz - 1) : (q + 1) * (nz - 1)]:
            copy.wait_recv()
        loop(tiles * q, tiles * (q + 1), pack_field, unroll=4)

    halo = [
        remote(F.at[:, :, p_first], F.at[:, :, below], north),
        remote(F.at[:, :, p_last], F.at[:, :, above], south),
    ]
    halo += send_columns(FMR, FML, FRL, FRR)
    for copy in swap + forward + arrived:
        copy.wait_send()
    for q in range(parts):
        for copy in spread[q] + list(gather[q].values()):
            copy.wait_send()

    inv_two_cells = 1.0 / (2.0 * CELL_SIZE)

    def flow(up, down, left, right, speed):
        gx = (down - up) * inv_two_cells
        gy = (right - left) * inv_two_cells
        scale = speed * lax.rsqrt(1.0 + gx * gx + gy * gy)
        return -scale * gx, -scale * gy

    def sides(row, h):
        left, right = roll(row[h], 1), roll(row[h], -1)
        if h > 0:
            left = jnp.where(lane == 0, roll(row[h - 1], 1), left)
        if h < halves - 1:
            right = jnp.where(lane == LANES - 1, roll(row[h + 1], -1), right)
        return left, right

    def three(base):
        return tile_at(base), pl.ds(base - 1, 8), pl.ds(base + 1, 8)

    def flows(i):
        t, tu, td = three(PAD - 8 + 8 * i)
        speed = []
        for h in range(halves):
            total = functools.reduce(jnp.add, [D[k, h, t] for k in range(groups)])
            speed.append(1.0 / (1.0 + total))
        for k in range(groups):
            centre = [F[k, h, t] for h in range(halves)]
            for h in range(halves):
                left, right = sides(centre, h)
                Vx[k, h, t], Vy[k, h, t] = flow(F[k, h, tu], F[k, h, td], left, right, speed[h])

    def strip_flows(i):
        t, tu, td = three(PAD - 8 + 8 * i)
        for side in (0, 1):
            d = Ds[side, t]
            d = d + roll(d, 32)
            d = d + roll(d, 64)
            c = Fs[side, t]
            Vxs[side, t], Vys[side, t] = flow(
                Fs[side, tu], Fs[side, td], roll(c, 1), roll(c, -1), 1.0 / (1.0 + d)
            )

    def flux(low_v, high_v, low_d, high_d):
        face = 0.5 * (low_v + high_v)
        return jnp.maximum(face, 0.0) * low_d + jnp.minimum(face, 0.0) * high_d

    def updated(i, vx, vxu, vxd, vy, vyl, vyr, d, du, dd, dl, dr, no_left, no_right):
        row = sub + 8 * i
        up = jnp.where(at_top & (row == 0), 0.0, flux(vxu, vx, du, d))
        down = jnp.where(at_bottom & (row == height - 1), 0.0, flux(vx, vxd, d, dd))
        left, right = flux(vyl, vy, dl, d), flux(vy, vyr, d, dr)
        left = left if no_left is None else jnp.where(no_left, 0.0, left)
        right = right if no_right is None else jnp.where(no_right, 0.0, right)
        return d - COURANT * (down - up + right - left)

    def advect(i):
        t, tu, td = three(PAD + 8 * i)
        for k in range(groups):
            vy = [Vy[k, h, t] for h in range(halves)]
            d = [D[k, h, t] for h in range(halves)]
            for h in range(halves):
                vyl, vyr = sides(vy, h)
                dl, dr = sides(d, h)
                DO[k, h, tile_at(8 * i)] = updated(
                    i, Vx[k, h, t], Vx[k, h, tu], Vx[k, h, td], vy[h], vyl, vyr,
                    d[h], D[k, h, tu], D[k, h, td], dl, dr, None, None,
                )

    def strip_advect(i):
        t, tu, td = three(PAD + 8 * i)
        to = tile_at(8 * i)
        strips = []
        for side in (0, 1):
            vx, vy, d = Vxs[side, t], Vys[side, t], Ds[side, t]
            new = updated(
                i, vx, Vxs[side, tu], Vxs[side, td], vy, roll(vy, 1), roll(vy, -1),
                d, Ds[side, tu], Ds[side, td], roll(d, 1), roll(d, -1),
                (at_left & (offset == 8)) if side == 0 else None,
                (at_right & (offset == 23)) if side == 1 else None,
            )
            strips.append((vx, vy, new))
        for k in range(groups):
            for h in range(halves):
                Vx[k, h, t] = merged(Vx[k, h, t], strips[0][0], strips[1][0], k, h)
                Vy[k, h, t] = merged(Vy[k, h, t], strips[0][1], strips[1][1], k, h)
                DO[k, h, to] = merged(DO[k, h, to], strips[0][2], strips[1][2], k, h)

    loop(2, n_ext - 2, flows, unroll=2)
    loop(2, height // 8 - 2, advect, unroll=2)
    for copy in halo:
        copy.wait()

    for flag, ghost, inner in ((at_top, above, PAD), (at_bottom, below, bottom - 1)):
        for h in range(halves):
            for k in range(groups):
                beside = jnp.broadcast_to(F[k, h, inner : inner + 1], (8, LANES))
                F[k, h, ghost] = jnp.where(flag, beside, F[k, h, ghost])

    def build_field(i):
        t = tile_at(PAD - 8 + 8 * i)
        f = jnp.where(own_left, in_slots([F[k, 0, t] for k in range(groups)], 8), FRL[t])
        Fs[0, t] = jnp.where(at_left & ~own_left, roll(f, -1), f)
        f = jnp.where(
            own_right, in_slots([F[k, halves - 1, t] for k in range(groups)], 24 - LANES), FRR[t]
        )
        Fs[1, t] = jnp.where(at_right & ~own_right, roll(f, 1), f)

    loop(0, n_ext, build_field, unroll=6)
    for flag, ghost, inner in ((at_top, above, PAD), (at_bottom, below, bottom - 1)):
        for side in (0, 1):
            beside = jnp.broadcast_to(Fs[side, inner : inner + 1], (8, LANES))
            Fs[side, ghost] = jnp.where(flag, beside, Fs[side, ghost])
    loop(0, n_ext, strip_flows, unroll=6)
    for i in (0, 1, n_ext - 2, n_ext - 1):
        flows(i)
    for i in (0, 1, height // 8 - 2, height // 8 - 1):
        advect(i)
    for q in range(parts):
        loop(tiles * q, tiles * (q + 1), strip_advect, unroll=2)
        rows, here = pl.ds(PAD + part * q, part), part_rows(q)
        for h in range(halves):
            outs.append(local(Vx.at[:, h, rows], vel_out.at[:, 0, here, cut[h]]))
            outs.append(local(Vy.at[:, h, rows], vel_out.at[:, 1, here, cut[h]]))
            outs.append(local(DO.at[:, h, here], den_out.at[:, here, cut[h]]))
    for copy in outs:
        copy.wait()


def solution(mesh):
    nx, ny, ng = mesh.shape["gx"], mesh.shape["gy"], mesh.shape["goal"]

    def per_device(potential, cost, obstacle, density, destinations, group_ids):
        goals, height, width = potential.shape
        groups = density.shape[0]
        halves = width // LANES
        rows = height + 2 * PAD
        nz = ng // 2
        f32 = jnp.float32

        def vm(*shape, dtype=f32):
            return pltpu.VMEM(shape, dtype)

        panel = (rows, LANES)
        flat = (height, LANES)
        scratch = [
            vm(goals, halves, *panel), vm(goals, halves, *panel), vm(2, *panel), vm(2, *panel), vm(halves, *panel), vm(2, *panel),
            vm(halves, *flat), vm(halves, *flat, dtype=jnp.int32),
            vm(groups, halves, *panel), vm(2, *panel), vm(*flat), vm(*flat), vm(*panel), vm(*panel),
            vm(groups, halves, *flat), vm(groups, *flat), vm(groups, *flat),
            vm(2, nz, groups, height // (2 * nz), LANES), vm(groups, halves, *panel), vm(2, *panel),
            vm(*flat), vm(*flat), vm(*panel), vm(*panel),
            vm(groups, halves, *panel), vm(groups, halves, *panel), vm(2, *panel), vm(2, *panel),
            vm(groups, halves, *flat),
            pltpu.SemaphoreType.DMA((32,)),
            pltpu.SemaphoreType.DMA((80,)),
            pltpu.SemaphoreType.DMA((80,)),
        ]
        anywhere = pl.BlockSpec(memory_space=pltpu.HBM)
        scalars = pl.BlockSpec(memory_space=pltpu.SMEM)
        return pl.pallas_call(
            functools.partial(kernel, nx, ny, nz, goals, groups, height, width),
            out_shape=(
                jax.ShapeDtypeStruct(potential.shape, f32),
                jax.ShapeDtypeStruct((groups, 2, height, width), f32),
                jax.ShapeDtypeStruct(density.shape, f32),
            ),
            in_specs=[anywhere] * 4 + [scalars] * 2,
            out_specs=(anywhere,) * 3,
            scratch_shapes=scratch,
            compiler_params=pltpu.CompilerParams(
                collective_id=0, has_side_effects=True, vmem_limit_bytes=67043328
            ),
            name="crowd_step",
        )(potential, cost, obstacle, density, destinations, group_ids)

    in_specs = (
        P("goal", "gx", "gy"),
        P("gx", "gy"),
        P("gx", "gy"),
        P(None, "gx", "gy"),
        P("goal"),
        P("goal"),
    )
    out_specs = (P("goal", "gx", "gy"), P(None, None, "gx", "gy"), P(None, "gx", "gy"))
    return jax.shard_map(
        per_device, mesh=mesh, in_specs=in_specs, out_specs=out_specs, check_vma=False
    )
```

time: 88.2 us -> 62.7 us (0.71)
  Pallas kernels: 79.5 us -> 57.6 us
  local copies, waits for them, and re-layouts: 7.75 us -> 4.15 us
    pallas_call x1, Pallas kernels: 79.5 us -> 57.6 us  [per_device(): pl.pallas_call(functools.partial(kernel, nx, ny, nz, goals, groups, heigh...]
    unnamed x15 -> x7, local copies, waits for them, and re-layouts: 7.75 us -> 4.15 us
where the time goes in v2:
time: 62.7 us; the launch traced here: 62.4 us
  Pallas kernels  57.6 us (92%)
  local copies, waits for them, and re-layouts  4.15 us (7%)
  between operations  0.65 us (1%)
    pallas_call x1, Pallas kernels, per_device(): pl.pallas_call(functools.partial(kernel, nx, ny, nz, goals, groups, heigh...  57.6 us
    unnamed x7, local copies, waits for them, and re-layouts  4.15 us

profile of v2, /device:TPU:1, one launch (start us, length us, event | category | flops | bytes accessed | tf_op | source)
XLA Modules:
  0.0 62.4 jit_solution(10084951192040981527)
XLA Ops:
  0.6 57.6 %crowd_step.1 = (f32[4,128,256]{2,1,0:T(8,128)}, f32[4,2,128,256]{3,2,1,0:T(8,128)}, f32[4,128,256]{2,1,0:T(8,128)}) custom-call(f32[4,128,256]{2,1,0:T(8,128)} %pot.1, f32[128,256]{1,0:T(8,128)} %cost.1, s32[128,256]{1,0:T(8,128)} %obst.1, f32[4,128,256]{2,1,0:T(8,128)} %dens.1, s32[4]{0:T(128)} %dest.1, s32[4]{0:T(128)} %gid.1), custom_call_target="tpu_custom_call" | custom-call | tf_op jit(solution)/shard_map/crowd_step/pallas_call | solution.py:531
  58.3 0.0 copy-start
  58.3 2.0 %copy.12 = f32[4,128,256]{2,1,0:T(8,128)} copy(f32[4,128,256]{2,1,0:T(8,128)} %get-tuple-element.6) | data formatting | bytes 1048576
  60.2 0.0 copy-done
  60.2 0.0 copy-start.1
  60.2 1.0 %copy.13 = f32[4,2,128,256]{3,2,1,0:T(8,128)} copy(f32[4,2,128,256]{3,2,1,0:T(8,128)S(1)} %copy-done) | data formatting | bytes 2097152
  61.2 0.4 copy-done.1
  61.6 0.8 %copy.14 = f32[4,128,256]{2,1,0:T(8,128)} copy(f32[4,128,256]{2,1,0:T(8,128)S(1)} %copy-done.1) | data formatting | bytes 1048576
Async XLA Ops:
  58.3 2.0 %copy-start = (f32[4,2,128,256]{3,2,1,0:T(8,128)S(1)}, f32[4,2,128,256]{3,2,1,0:T(8,128)}, u32[]{:S(2)}) copy-start(f32[4,2,128,256]{3,2,1,0:T(8,128)} %get-tuple-element.7) | copy-start | bytes 3145732
  60.2 1.4 %copy-start.1 = (f32[4,128,256]{2,1,0:T(8,128)S(1)}, f32[4,128,256]{2,1,0:T(8,128)}, u32[]{:S(2)}) copy-start(f32[4,128,256]{2,1,0:T(8,128)} %get-tuple-element.8) | copy-start | bytes 1572868

commit v3 on v2

--- a/solution.py
+++ b/solution.py
@@ -22,6 +22,7 @@
 LANES = 128
 PAD = 16
 U_SWEEP, U_BUILD, U_FIN = 9, 3, 4
+VMEM_LIMIT = 67043328 - (2 << 20) - (64 << 10)
 K_SWEEP = float(1.0 / (SWEEP_TEMP * np.log(2.0)))
 K_GOAL = float(1.0 / (GOAL_TEMP * np.log(2.0)))
 
@@ -114,8 +115,6 @@
     for h in range(halves):
         halo.append(remote(pot.at[:, first, cut[h]], XA.at[:, h, below], north))
         halo.append(remote(pot.at[:, last, cut[h]], XA.at[:, h, above], south))
-        halo.append(remote(dens.at[:, first, cut[h]], D.at[:, h, below], north))
-        halo.append(remote(dens.at[:, last, cut[h]], D.at[:, h, above], south))
 
     lane = lax.broadcasted_iota(jnp.int32, (8, LANES), 1)
     sub = lax.broadcasted_iota(jnp.int32, (8, LANES), 0)
@@ -186,35 +185,92 @@
         return out
 
     halo += send_columns(MR, ML, RL, RR)
-    for copy in halo:
-        copy.wait()
+    late = []
+    for h in range(halves):
+        late.append(remote(dens.at[:, first, cut[h]], D.at[:, h, below], north))
+        late.append(remote(dens.at[:, last, cut[h]], D.at[:, h, above], south))
 
     n_ext = height // 8 + 2
     own_left, own_right = offset >= 8, offset < 24
+
+    def build_own(i):
+        t = tile_at(PAD - 8 + 8 * i)
+        SA[0, t] = in_slots([XA[g, 0, t] for g in range(goals)], 8)
+        SA[1, t] = in_slots([XA[g, halves - 1, t] for g in range(goals)], 24 - LANES)
 
     def build(i):
         t = tile_at(PAD - 8 + 8 * i)
         from_left, from_right = RL[t], RR[t]
         s = jnp.where(own_left, in_slots([S[0, t]] * goals, 8), roll(from_left, -8))
         s_left = jnp.where(at_left & ~own_left, SHUT, s)
-        p = jnp.where(own_left, in_slots([XA[g, 0, t] for g in range(goals)], 8), from_left)
+        p = jnp.where(own_left, SA[0, t], from_left)
         SA[0, t] = jnp.where(at_left & ~own_left, FAR - roll(s, -1), p)
         Ss[0, t] = s_left
-        Ds[0, t] = jnp.where(
-            own_left, in_slots([D[k, 0, t] for k in range(groups)], 8), roll(from_left, -16)
-        )
         shift = 24 - LANES
         s = jnp.where(own_right, in_slots([S[halves - 1, t]] * goals, shift), roll(from_right, 8))
         s_right = jnp.where(at_right & ~own_right, SHUT, s)
-        p = jnp.where(
-            own_right, in_slots([XA[g, halves - 1, t] for g in range(goals)], shift), from_right
-        )
+        p = jnp.where(own_right, SA[1, t], from_right)
         SA[1, t] = jnp.where(at_right & ~own_right, FAR - roll(s, 1), p)
         Ss[1, t] = s_right
-        Ds[1, t] = jnp.where(
-            own_right, in_slots([D[k, halves - 1, t] for k in range(groups)], shift), roll(from_right, 16)
-        )
-
+
+    width_all = width * ny
+    cell = sub * width + lane
+    target, strip_row = [], [jnp.full((8, LANES), -1000, jnp.int32) for _ in (0, 1)]
+    for g in range(goals):
+        row = dest[g] // width_all - ix * height
+        col = dest[g] % width_all - iy * width
+        held = (col >= 0) & (col < width)
+        target.append(jnp.where(held, row * width + col, -(1 << 24)))
+        for side, start in ((0, -8), (1, width - 24)):
+            here = (slot == g) & (offset + start == col)
+            strip_row[side] = jnp.where(here, row, strip_row[side])
+
+    def relax(centre, up, down, left, right, s):
+        return soft_min([centre, up + s, down + s, left + s, right + s], K_SWEEP, SWEEP_TEMP)
+
+    def three(base):
+        return tile_at(base), pl.ds(base - 1, 8), pl.ds(base + 1, 8)
+
+    def sweep(number, lo, hi, main, strips):
+        now, later = (number - 1) % 2, number % 2
+
+        def tile(i):
+            t, tu, td = three(PAD - 8 + 8 * i)
+            row = 8 * i - 8
+            if main:
+                s = [S[h, t] for h in range(halves)]
+                for g in range(goals):
+                    centre = [X[now][g, h, t] for h in range(halves)]
+                    to_right = [roll(c, 1) for c in centre]
+                    to_left = [roll(c, -1) for c in centre]
+                    for h in range(halves):
+                        left, right = to_right[h], to_left[h]
+                        if h > 0:
+                            left = jnp.where(lane == 0, to_right[h - 1], left)
+                        if h < halves - 1:
+                            right = jnp.where(lane == LANES - 1, to_left[h + 1], right)
+                        new = relax(centre[h], X[now][g, h, tu], X[now][g, h, td], left, right, s[h])
+                        pinned = cell == target[g] - (row * width + LANES * h)
+                        X[later][g, h, t] = jnp.where(pinned, 0.0, new)
+            if strips:
+                for side in (0, 1):
+                    c = St[now][side, t]
+                    new = relax(
+                        c, St[now][side, tu], St[now][side, td], roll(c, 1), roll(c, -1), Ss[side, t]
+                    )
+                    St[later][side, t] = jnp.where(strip_row[side] == sub + row, 0.0, new)
+
+        if hi > lo:
+            loop(lo, hi, tile, unroll=hi - lo)
+
+    loop(1, n_ext - 1, build_own, unroll=4)
+    early = 3
+    for number in range(1, early + 1):
+        sweep(number, number + 1, n_ext - 1 - number, True, False)
+    for copy in halo:
+        copy.wait()
+    build_own(0)
+    build_own(n_ext - 1)
     loop(0, n_ext, build, unroll=U_BUILD)
 
     for flag, ghost, inner in ((at_top, above, PAD), (at_bottom, below, bottom - 1)):
@@ -230,52 +286,16 @@
             SA[side, ghost] = jnp.where(flag, beside, SA[side, ghost])
             Ss[side, ghost] = jnp.where(flag, SHUT, Ss[side, ghost])
 
-    width_all = width * ny
-    cell = sub * width + lane
-    target, strip_row = [], [jnp.full((8, LANES), -1000, jnp.int32) for _ in (0, 1)]
-    for g in range(goals):
-        row = dest[g] // width_all - ix * height
-        col = dest[g] % width_all - iy * width
-        held = (col >= 0) & (col < width)
-        target.append(jnp.where(held, row * width + col, -(1 << 24)))
-        for side, start in ((0, -8), (1, width - 24)):
-            here = (slot == g) & (offset + start == col)
-            strip_row[side] = jnp.where(here, row, strip_row[side])
-
-    def relax(centre, up, down, left, right, s):
-        return soft_min([centre, up + s, down + s, left + s, right + s], K_SWEEP, SWEEP_TEMP)
-
-    def sweep(now, later, lo, hi):
-        def tile(i):
-            base = PAD - 8 + 8 * i
-            t, tu, td = tile_at(base), pl.ds(base - 1, 8), pl.ds(base + 1, 8)
-            row = 8 * i - 8
-            s = [S[h, t] for h in range(halves)]
-            for g in range(goals):
-                centre = [X[now][g, h, t] for h in range(halves)]
-                to_right = [roll(c, 1) for c in centre]
-                to_left = [roll(c, -1) for c in centre]
-                for h in range(halves):
-                    left, right = to_right[h], to_left[h]
-                    if h > 0:
-                        left = jnp.where(lane == 0, to_right[h - 1], left)
-                    if h < halves - 1:
-                        right = jnp.where(lane == LANES - 1, to_left[h + 1], right)
-                    new = relax(centre[h], X[now][g, h, tu], X[now][g, h, td], left, right, s[h])
-                    pinned = cell == target[g] - (row * width + LANES * h)
-                    X[later][g, h, t] = jnp.where(pinned, 0.0, new)
-            for side in (0, 1):
-                c = St[now][side, t]
-                new = relax(c, St[now][side, tu], St[now][side, td], roll(c, 1), roll(c, -1), Ss[side, t])
-                St[later][side, t] = jnp.where(strip_row[side] == sub + row, 0.0, new)
-
-        loop(lo, hi, tile, unroll=U_SWEEP)
-
-    def two_sweeps(j):
-        sweep(0, 1, 0, n_ext)
-        sweep(1, 0, 0, n_ext)
-
-    loop(0, SWEEPS // 2, two_sweeps)
+    for number in range(1, SWEEPS + 1):
+        start, stop = (1 if number == SWEEPS else 0), n_ext - 1 - number
+        if number <= early:
+            sweep(number, start, number + 1, True, True)
+            sweep(number, number + 1, stop, False, True)
+        else:
+            sweep(number, start, stop, True, True)
+
+    def lower(number):
+        sweep(number, n_ext - 1 - number, n_ext - (1 if number == SWEEPS else 0), True, True)
 
     bias = [[jnp.where(gid[g] == k, 0.0, ABSENT) for k in range(groups)] for g in range(goals)]
 
@@ -292,7 +312,7 @@
         for h in range(halves):
             p = [merged(XA[g, h, t], strips[0], strips[1], g, h) for g in range(goals)]
             for g in range(goals):
-                XA[g, h, t] = p[g]
+                pot_out[g, tile_at(8 * i), cut[h]] = p[g]
             for k in range(groups):
                 G[k, h, tile_at(8 * i)] = soft_min(
                     [p[g] + bias[g][k] for g in range(goals)], K_GOAL, GOAL_TEMP
@@ -301,15 +321,15 @@
     parts = 2
     part = height // parts
     tiles = part // 8
-    outs, swap, spread, gather, forward = [], [], [], [], []
+    swap, spread, gather, forward = [], [], [], []
 
     def part_rows(q):
         return pl.ds(part * q, part)
 
-    for q in range(parts):
+    def finish_part(q):
         loop(tiles * q, tiles * (q + 1), finish, unroll=U_FIN)
         swap.append(remote(G.at[:, 1 - core, part_rows(q)], G2.at[:, part_rows(q)], partner))
-    outs += [local(XA.at[:, h, body_rows], pot_out.at[:, :, cut[h]]) for h in range(halves)]
+
 
     def join(i):
         t = tile_at(8 * i)
@@ -322,10 +342,17 @@
         return pl.ds(pl.multiple_of(part * q + chunk * j, 8), chunk)
 
     order = sorted(range(1, nz), key=lambda d: -min(d, nz - d))
+    finish_part(0)
+    for number in range(1, SWEEPS - 1):
+        lower(number)
     for q in range(parts):
         swap[q].wait_recv()
-        loop(tiles * q, tiles * (q + 1), join, unroll=2)
+        loop(tiles * q, tiles * (q + 1), join, unroll=4)
         spread.append([remote(H.at[:, block(q, z_at[d])], R.at[q, d], z_peer[d]) for d in order])
+        if q == 0:
+            lower(SWEEPS - 1)
+            lower(SWEEPS)
+            finish_part(1)
 
     def mine(q, j):
         return F.at[:, core, pl.ds(pl.multiple_of(PAD + part * q + chunk * j, 8), chunk)]
@@ -384,9 +411,6 @@
         if h < halves - 1:
             right = jnp.where(lane == LANES - 1, roll(row[h + 1], -1), right)
         return left, right
-
-    def three(base):
-        return tile_at(base), pl.ds(base - 1, 8), pl.ds(base + 1, 8)
 
     def flows(i):
         t, tu, td = three(PAD - 8 + 8 * i)
@@ -452,12 +476,22 @@
             strips.append((vx, vy, new))
         for k in range(groups):
             for h in range(halves):
-                Vx[k, h, t] = merged(Vx[k, h, t], strips[0][0], strips[1][0], k, h)
-                Vy[k, h, t] = merged(Vy[k, h, t], strips[0][1], strips[1][1], k, h)
-                DO[k, h, to] = merged(DO[k, h, to], strips[0][2], strips[1][2], k, h)
+                vel_out[k, 0, to, cut[h]] = merged(Vx[k, h, t], strips[0][0], strips[1][0], k, h)
+                vel_out[k, 1, to, cut[h]] = merged(Vy[k, h, t], strips[0][1], strips[1][1], k, h)
+                den_out[k, to, cut[h]] = merged(DO[k, h, to], strips[0][2], strips[1][2], k, h)
+
+    def build_density(i):
+        t = tile_at(PAD - 8 + 8 * i)
+        own = in_slots([D[k, 0, t] for k in range(groups)], 8)
+        Ds[0, t] = jnp.where(own_left, own, roll(RL[t], -16))
+        own = in_slots([D[k, halves - 1, t] for k in range(groups)], 24 - LANES)
+        Ds[1, t] = jnp.where(own_right, own, roll(RR[t], 16))
 
     loop(2, n_ext - 2, flows, unroll=2)
     loop(2, height // 8 - 2, advect, unroll=2)
+    for copy in late:
+        copy.wait()
+    loop(0, n_ext, build_density, unroll=6)
     for copy in halo:
         copy.wait()
 
@@ -486,15 +520,7 @@
         flows(i)
     for i in (0, 1, height // 8 - 2, height // 8 - 1):
         advect(i)
-    for q in range(parts):
-        loop(tiles * q, tiles * (q + 1), strip_advect, unroll=2)
-        rows, here = pl.ds(PAD + part * q, part), part_rows(q)
-        for h in range(halves):
-            outs.append(local(Vx.at[:, h, rows], vel_out.at[:, 0, here, cut[h]]))
-            outs.append(local(Vy.at[:, h, rows], vel_out.at[:, 1, here, cut[h]]))
-            outs.append(local(DO.at[:, h, here], den_out.at[:, here, cut[h]]))
-    for copy in outs:
-        copy.wait()
+    loop(0, height // 8, strip_advect, unroll=2)
 
 
 def solution(mesh):
@@ -531,15 +557,15 @@
         return pl.pallas_call(
             functools.partial(kernel, nx, ny, nz, goals, groups, height, width),
             out_shape=(
-                jax.ShapeDtypeStruct(potential.shape, f32),
-                jax.ShapeDtypeStruct((groups, 2, height, width), f32),
-                jax.ShapeDtypeStruct(density.shape, f32),
+                vm(*potential.shape),
+                vm(groups, 2, height, width),
+                vm(*density.shape),
             ),
             in_specs=[anywhere] * 4 + [scalars] * 2,
-            out_specs=(anywhere,) * 3,
+            out_specs=(pl.BlockSpec(memory_space=pltpu.VMEM),) * 3,
             scratch_shapes=scratch,
             compiler_params=pltpu.CompilerParams(
-                collective_id=0, has_side_effects=True, vmem_limit_bytes=67043328
+                collective_id=0, has_side_effects=True, vmem_limit_bytes=VMEM_LIMIT
             ),
             name="crowd_step",
         )(potential, cost, obstacle, density, destinations, group_ids)

time: 62.7 us -> 55.5 us (0.89)
  Pallas kernels: 57.6 us -> 52.2 us
  local copies, waits for them, and re-layouts: 4.15 us -> 2.56 us
    pallas_call x1, Pallas kernels: 57.6 us -> 52.2 us  [per_device(): pl.pallas_call(functools.partial(kernel, nx, ny, nz, goals, groups, heigh...]
    unnamed x7 -> x3, local copies, waits for them, and re-layouts: 4.15 us -> 2.56 us
where the time goes in v3:
time: 55.5 us; the launch traced here: 55.4 us
  Pallas kernels  52.2 us (94%)
  local copies, waits for them, and re-layouts  2.56 us (5%)
  between operations  0.64 us (1%)
    pallas_call x1, Pallas kernels, per_device(): pl.pallas_call(functools.partial(kernel, nx, ny, nz, goals, groups, heigh...  52.2 us
    unnamed x3, local copies, waits for them, and re-layouts  2.56 us

profile of v3, /device:TPU:1, one launch (start us, length us, event | category | flops | bytes accessed | tf_op | source)
XLA Modules:
  0.0 55.4 jit_solution(7425290381327831646)
XLA Ops:
  0.6 52.2 %crowd_step.1 = (f32[4,128,256]{2,1,0:T(8,128)S(1)}, f32[4,2,128,256]{3,2,1,0:T(8,128)S(1)}, f32[4,128,256]{2,1,0:T(8,128)S(1)}) custom-call(f32[4,128,256]{2,1,0:T(8,128)} %pot.1, f32[128,256]{1,0:T(8,128)} %cost.1, s32[128,256]{1,0:T(8,128)} %obst.1, f32[4,128,256]{2,1,0:T(8,128)} %dens.1, s32[4]{0:T(128)} %dest.1, s32[4]{0:T(128)} %gid.1), custom_call_target="tpu_custom_call" | custom-call | tf_op jit(solution)/shard_map/crowd_step/pallas_call | solution.py:557
  52.8 0.8 %copy.12 = f32[4,128,256]{2,1,0:T(8,128)} copy(f32[4,128,256]{2,1,0:T(8,128)S(1)} %get-tuple-element.3) | data formatting | bytes 1048576
  53.6 0.8 %copy.14 = f32[4,128,256]{2,1,0:T(8,128)} copy(f32[4,128,256]{2,1,0:T(8,128)S(1)} %get-tuple-element.5) | data formatting | bytes 1048576
  54.4 1.0 %copy.13 = f32[4,2,128,256]{3,2,1,0:T(8,128)} copy(f32[4,2,128,256]{3,2,1,0:T(8,128)S(1)} %get-tuple-element.4) | data formatting | bytes 2097152

commit v4 on v3

--- a/solution.py
+++ b/solution.py
@@ -52,11 +52,11 @@
 
 def kernel(
     nx, ny, nz, goals, groups, height, width,
-    pot, cost, obst, dens, dest, gid,
+    pot, cost, obst, dens, dest_in, gid_in,
     pot_out, vel_out, den_out,
     XA, XB, SA, SB, S, Ss, Cb, Ob, D, Ds, ML, MR, RL, RR,
     G, G2, H, R, F, Fs, FML, FMR, FRL, FRR, Vx, Vy, Vxs, Vys, DO,
-    lsem, ssem, rsem,
+    dest, gid, DML, DMR, DRL, DRR, lsem, ssem, rsem,
 ):
     X, St = (XA, XB), (SA, SB)
     halves = width // LANES
@@ -96,7 +96,8 @@
     cost_in = [local(cost.at[:, cut[h]], Cb.at[h]) for h in range(halves)]
     cost_in += [local(obst.at[:, cut[h]], Ob.at[h]) for h in range(halves)]
     field_in = [local(pot.at[:, :, cut[h]], XA.at[:, h, body_rows]) for h in range(halves)]
-    field_in += [local(dens.at[:, :, cut[h]], D.at[:, h, body_rows]) for h in range(halves)]
+    scalars_in = [local(dest_in, dest), local(gid_in, gid)]
+    density_in = [local(dens.at[:, :, cut[h]], D.at[:, h, body_rows]) for h in range(halves)]
 
     sent = [0]
 
@@ -160,31 +161,37 @@
         tm = tile_at(8 * i)
         p = [XA[g, halves - 1, t] for g in range(goals)]
         s = [S[halves - 1, t]] * goals
-        d = [D[k, halves - 1, t] for k in range(groups)]
-        out = in_slots(p, right_edge)
-        out = jnp.where(offset < 8, out, in_slots(s, right_edge + 8))
-        MR[tm] = jnp.where(offset < 16, out, in_slots(d, right_edge + 16))
+        MR[tm] = jnp.where(offset < 8, in_slots(p, right_edge), in_slots(s, right_edge + 8))
         p = [XA[g, 0, t] for g in range(goals)]
         s = [S[0, t]] * goals
-        d = [D[k, 0, t] for k in range(groups)]
-        out = in_slots(p, 24)
-        out = jnp.where(offset >= 24, out, in_slots(s, 16))
-        ML[tm] = jnp.where(offset >= 16, out, in_slots(d, 8))
-
-    loop(0, height // 8, pack, unroll=2)
-
-    def send_columns(mr, ml, rl, rr):
-        out = [
-            remote(mr, rl.at[body_rows], (xs[0], ys[1], ig)),
-            remote(ml, rr.at[body_rows], (xs[0], ys[-1], ig)),
-            remote(mr.at[first], rl.at[below], (xs[-1], ys[1], ig)),
-            remote(mr.at[last], rl.at[above], (xs[1], ys[1], ig)),
-            remote(ml.at[first], rr.at[below], (xs[-1], ys[-1], ig)),
-            remote(ml.at[last], rr.at[above], (xs[1], ys[-1], ig)),
+        ML[tm] = jnp.where(offset >= 24, in_slots(p, 24), in_slots(s, 16))
+
+    loop(0, height // 8, pack, unroll=4)
+
+    def pack_columns(source, mr, ml):
+        def one(i):
+            t, tm = tile_at(PAD + 8 * i), tile_at(8 * i)
+            mr[tm] = in_slots([source[k, halves - 1, t] for k in range(groups)], right_edge)
+            ml[tm] = in_slots([source[k, 0, t] for k in range(groups)], 24)
+
+        return one
+
+    def send_sides(mr, ml, rl, rr, start, rows):
+        here, there = pl.ds(start, rows), pl.ds(PAD + start, rows)
+        return [
+            remote(mr.at[here], rl.at[there], (xs[0], ys[1], ig)),
+            remote(ml.at[here], rr.at[there], (xs[0], ys[-1], ig)),
         ]
-        return out
-
-    halo += send_columns(MR, ML, RL, RR)
+
+    def send_corners(mr, ml, rl, rr, dx):
+        here, there = (first, below) if dx < 0 else (last, above)
+        return [
+            remote(mr.at[here], rl.at[there], (xs[dx], ys[1], ig)),
+            remote(ml.at[here], rr.at[there], (xs[dx], ys[-1], ig)),
+        ]
+
+    halo += send_sides(MR, ML, RL, RR, 0, height)
+    halo += send_corners(MR, ML, RL, RR, -1) + send_corners(MR, ML, RL, RR, 1)
     late = []
     for h in range(halves):
         late.append(remote(dens.at[:, first, cut[h]], D.at[:, h, below], north))
@@ -213,6 +220,8 @@
         SA[1, t] = jnp.where(at_right & ~own_right, FAR - roll(s, 1), p)
         Ss[1, t] = s_right
 
+    for copy in scalars_in:
+        copy.wait()
     width_all = width * ny
     cell = sub * width + lane
     target, strip_row = [], [jnp.full((8, LANES), -1000, jnp.int32) for _ in (0, 1)]
@@ -327,8 +336,13 @@
         return pl.ds(part * q, part)
 
     def finish_part(q):
-        loop(tiles * q, tiles * (q + 1), finish, unroll=U_FIN)
-        swap.append(remote(G.at[:, 1 - core, part_rows(q)], G2.at[:, part_rows(q)], partner))
+        piece = part // 2
+        moves = []
+        for start in (part * q, part * q + piece):
+            loop(start // 8, (start + piece) // 8, finish, unroll=U_FIN)
+            rows = pl.ds(start, piece)
+            moves.append(remote(G.at[:, 1 - core, rows], G2.at[:, rows], partner))
+        swap.append(moves)
 
 
     def join(i):
@@ -346,13 +360,19 @@
     for number in range(1, SWEEPS - 1):
         lower(number)
     for q in range(parts):
-        swap[q].wait_recv()
-        loop(tiles * q, tiles * (q + 1), join, unroll=4)
+        for n, copy in enumerate(swap[q]):
+            copy.wait_recv()
+            loop(tiles * q + tiles // 2 * n, tiles * q + tiles // 2 * (n + 1), join, unroll=4)
         spread.append([remote(H.at[:, block(q, z_at[d])], R.at[q, d], z_peer[d]) for d in order])
         if q == 0:
             lower(SWEEPS - 1)
             lower(SWEEPS)
             finish_part(1)
+
+    for copy in density_in:
+        copy.wait()
+    loop(0, height // 8, pack_columns(D, DMR, DML), unroll=4)
+    late += send_sides(DMR, DML, DRL, DRR, 0, height)
 
     def mine(q, j):
         return F.at[:, core, pl.ds(pl.multiple_of(PAD + part * q + chunk * j, 8), chunk)]
@@ -368,33 +388,6 @@
                 F[k, core, tile_at(PAD + row)] = soft_min(items, K_GOAL, GOAL_TEMP)
         gather.append({d: remote(mine(q, z), mine(q, z), z_peer[d]) for d in order})
         forward.append(remote(mine(q, z), mine(q, z), partner))
-
-    def pack_field(i):
-        t = tile_at(PAD + 8 * i)
-        FMR[tile_at(8 * i)] = in_slots([F[k, halves - 1, t] for k in range(groups)], right_edge)
-        FML[tile_at(8 * i)] = in_slots([F[k, 0, t] for k in range(groups)], 24)
-
-    arrived = []
-    for q in range(parts):
-        for d in order[::-1]:
-            gather[q][d].wait_recv()
-            arrived.append(remote(mine(q, z_back[d]), mine(q, z_back[d]), partner))
-    for q in range(parts):
-        forward[q].wait_recv()
-        for copy in arrived[q * (nz - 1) : (q + 1) * (nz - 1)]:
-            copy.wait_recv()
-        loop(tiles * q, tiles * (q + 1), pack_field, unroll=4)
-
-    halo = [
-        remote(F.at[:, :, p_first], F.at[:, :, below], north),
-        remote(F.at[:, :, p_last], F.at[:, :, above], south),
-    ]
-    halo += send_columns(FMR, FML, FRL, FRR)
-    for copy in swap + forward + arrived:
-        copy.wait_send()
-    for q in range(parts):
-        for copy in spread[q] + list(gather[q].values()):
-            copy.wait_send()
 
     inv_two_cells = 1.0 / (2.0 * CELL_SIZE)
 
@@ -483,23 +476,9 @@
     def build_density(i):
         t = tile_at(PAD - 8 + 8 * i)
         own = in_slots([D[k, 0, t] for k in range(groups)], 8)
-        Ds[0, t] = jnp.where(own_left, own, roll(RL[t], -16))
+        Ds[0, t] = jnp.where(own_left, own, DRL[t])
         own = in_slots([D[k, halves - 1, t] for k in range(groups)], 24 - LANES)
-        Ds[1, t] = jnp.where(own_right, own, roll(RR[t], 16))
-
-    loop(2, n_ext - 2, flows, unroll=2)
-    loop(2, height // 8 - 2, advect, unroll=2)
-    for copy in late:
-        copy.wait()
-    loop(0, n_ext, build_density, unroll=6)
-    for copy in halo:
-        copy.wait()
-
-    for flag, ghost, inner in ((at_top, above, PAD), (at_bottom, below, bottom - 1)):
-        for h in range(halves):
-            for k in range(groups):
-                beside = jnp.broadcast_to(F[k, h, inner : inner + 1], (8, LANES))
-                F[k, h, ghost] = jnp.where(flag, beside, F[k, h, ghost])
+        Ds[1, t] = jnp.where(own_right, own, DRR[t])
 
     def build_field(i):
         t = tile_at(PAD - 8 + 8 * i)
@@ -510,17 +489,79 @@
         )
         Fs[1, t] = jnp.where(at_right & ~own_right, roll(f, 1), f)
 
-    loop(0, n_ext, build_field, unroll=6)
+    pack_field = pack_columns(F, FMR, FML)
+    halos = []
+
+    def collect(q):
+        arrived = []
+        for d in order[::-1]:
+            gather[q][d].wait_recv()
+            arrived.append(remote(mine(q, z_back[d]), mine(q, z_back[d]), partner))
+        for copy in [forward[q]] + arrived:
+            copy.wait_recv()
+        loop(tiles * q, tiles * (q + 1), pack_field, unroll=4)
+        if q == 0:
+            out = [remote(F.at[:, :, p_first], F.at[:, :, below], north)]
+            out += send_corners(FMR, FML, FRL, FRR, -1)
+        else:
+            out = [remote(F.at[:, :, p_last], F.at[:, :, above], south)]
+            out += send_corners(FMR, FML, FRL, FRR, 1)
+        halos.append(out + send_sides(FMR, FML, FRL, FRR, part * q, part))
+        return arrived
+
+    passed = collect(0)
+    loop(2, 8, flows, unroll=2)
+    loop(2, 6, advect, unroll=2)
+    passed += collect(1)
+    loop(8, n_ext - 2, flows, unroll=2)
+    loop(6, height // 8 - 2, advect, unroll=2)
+    for copy in late:
+        copy.wait()
+    loop(0, n_ext, build_density, unroll=6)
+    for copy in halos[0]:
+        copy.wait()
+    loop(1, 9, build_field, unroll=4)
+    loop(2, 8, strip_flows, unroll=6)
+    loop(2, 6, strip_advect, unroll=2)
+    for copy in halos[1]:
+        copy.wait()
+
+    for flag, ghost, inner in ((at_top, above, PAD), (at_bottom, below, bottom - 1)):
+        for h in range(halves):
+            for k in range(groups):
+                beside = jnp.broadcast_to(F[k, h, inner : inner + 1], (8, LANES))
+                F[k, h, ghost] = jnp.where(flag, beside, F[k, h, ghost])
+    build_field(0)
+    loop(9, n_ext, build_field, unroll=9)
     for flag, ghost, inner in ((at_top, above, PAD), (at_bottom, below, bottom - 1)):
         for side in (0, 1):
             beside = jnp.broadcast_to(Fs[side, inner : inner + 1], (8, LANES))
             Fs[side, ghost] = jnp.where(flag, beside, Fs[side, ghost])
-    loop(0, n_ext, strip_flows, unroll=6)
     for i in (0, 1, n_ext - 2, n_ext - 1):
         flows(i)
+    for i in (0, 1):
+        strip_flows(i)
+    loop(8, n_ext, strip_flows, unroll=10)
     for i in (0, 1, height // 8 - 2, height // 8 - 1):
         advect(i)
-    loop(0, height // 8, strip_advect, unroll=2)
+    loop(0, 2, strip_advect, unroll=2)
+    loop(6, height // 8, strip_advect, unroll=2)
+
+    for copy in swap[0] + swap[1] + forward + passed:
+        copy.wait_send()
+    for q in range(parts):
+        for copy in spread[q] + list(gather[q].values()):
+            copy.wait_send()
+
+
+def settle(*refs):
+    *ends, sem = refs
+    n = len(ends) // 2
+    copies = [pltpu.make_async_copy(ends[i], ends[n + i], sem.at[i]) for i in range(n)]
+    for copy in copies:
+        copy.start()
+    for copy in copies:
+        copy.wait()
 
 
 def solution(mesh):
@@ -548,20 +589,21 @@
             vm(*flat), vm(*flat), vm(*panel), vm(*panel),
             vm(groups, halves, *panel), vm(groups, halves, *panel), vm(2, *panel), vm(2, *panel),
             vm(groups, halves, *flat),
+            pltpu.SMEM((goals,), jnp.int32), pltpu.SMEM((goals,), jnp.int32),
+            vm(*flat), vm(*flat), vm(*panel), vm(*panel),
             pltpu.SemaphoreType.DMA((32,)),
-            pltpu.SemaphoreType.DMA((80,)),
-            pltpu.SemaphoreType.DMA((80,)),
+            pltpu.SemaphoreType.DMA((88,)),
+            pltpu.SemaphoreType.DMA((88,)),
         ]
         anywhere = pl.BlockSpec(memory_space=pltpu.HBM)
-        scalars = pl.BlockSpec(memory_space=pltpu.SMEM)
-        return pl.pallas_call(
+        results = pl.pallas_call(
             functools.partial(kernel, nx, ny, nz, goals, groups, height, width),
             out_shape=(
                 vm(*potential.shape),
                 vm(groups, 2, height, width),
                 vm(*density.shape),
             ),
-            in_specs=[anywhere] * 4 + [scalars] * 2,
+            in_specs=[anywhere] * 6,
             out_specs=(pl.BlockSpec(memory_space=pltpu.VMEM),) * 3,
             scratch_shapes=scratch,
             compiler_params=pltpu.CompilerParams(
@@ -569,6 +611,15 @@
             ),
             name="crowd_step",
         )(potential, cost, obstacle, density, destinations, group_ids)
+        return pl.pallas_call(
+            settle,
+            out_shape=tuple(jax.ShapeDtypeStruct(r.shape, f32) for r in results),
+            in_specs=[pl.BlockSpec(memory_space=pltpu.VMEM)] * 3,
+            out_specs=(pl.BlockSpec(memory_space=pltpu.HBM),) * 3,
+            scratch_shapes=[pltpu.SemaphoreType.DMA((3,))],
+            compiler_params=pltpu.CompilerParams(vmem_limit_bytes=1 << 20),
+            name="settle",
+        )(*results)
 
     in_specs = (
         P("goal", "gx", "gy"),

time: 55.5 us -> 51 us (0.919)
  local copies, waits for them, and re-layouts: 2.56 us -> 0 us
  Pallas kernels: 52.2 us -> 50.2 us
    pallas_call x1, Pallas kernels: 52.2 us -> 48.9 us  [per_device(): pl.pallas_call(functools.partial(kernel, nx, ny, nz, goals, groups, heigh...]
    unnamed x3 -> x0, local copies, waits for them, and re-layouts: 2.56 us -> none
    pallas_call x0 -> x1, Pallas kernels: none -> 1.34 us  [per_device(): pl.pallas_call(settle, out_shape=tuple((jax.ShapeDtypeStruct(r.shape, f32...]
where the time goes in v4:
time: 51 us; the launch traced here: 50.9 us
  Pallas kernels  50.2 us (98%)
  between operations  0.64 us (1%)
    pallas_call x1, Pallas kernels, per_device(): pl.pallas_call(functools.partial(kernel, nx, ny, nz, goals, groups, heigh...  48.9 us
    pallas_call x1, Pallas kernels, per_device(): pl.pallas_call(settle, out_shape=tuple((jax.ShapeDtypeStruct(r.shape, f32...  1.34 us

profile of v4, /device:TPU:1, one launch (start us, length us, event | category | flops | bytes accessed | tf_op | source)
XLA Modules:
  0.0 50.9 jit_solution(2787514703614979758)
XLA Ops:
  0.6 48.9 %crowd_step.1 = (f32[4,128,256]{2,1,0:T(8,128)S(1)}, f32[4,2,128,256]{3,2,1,0:T(8,128)S(1)}, f32[4,128,256]{2,1,0:T(8,128)S(1)}) custom-call(f32[4,128,256]{2,1,0:T(8,128)} %pot.1, f32[128,256]{1,0:T(8,128)} %cost.1, s32[128,256]{1,0:T(8,128)} %obst.1, f32[4,128,256]{2,1,0:T(8,128)} %dens.1, s32[4]{0:T(128)} %dest_in.1, s32[4]{0:T(128)} %gid_in.1), custom_call_target="tpu_custom_call" | custom-call | tf_op jit(solution)/shard_map/crowd_step/pallas_call | solution.py:599
  49.5 1.3 %settle.1 = (f32[4,128,256]{2,1,0:T(8,128)}, f32[4,2,128,256]{3,2,1,0:T(8,128)}, f32[4,128,256]{2,1,0:T(8,128)}) custom-call(f32[4,128,256]{2,1,0:T(8,128)S(1)} %get-tuple-element.6.refs_0_, f32[4,2,128,256]{3,2,1,0:T(8,128)S(1)} %get-tuple-element.7.refs_1_, f32[4,128,256]{2,1,0:T(8,128)S(1)} %get-tuple-element.8.refs_2_), custom_call_target="tpu_custom_call" | custom-call | tf_op jit(solution)/shard_map/settle/pallas_call | solution.py:614

commit v5 on v4

--- a/solution.py
+++ b/solution.py
@@ -55,7 +55,7 @@
     pot, cost, obst, dens, dest_in, gid_in,
     pot_out, vel_out, den_out,
     XA, XB, SA, SB, S, Ss, Cb, Ob, D, Ds, ML, MR, RL, RR,
-    G, G2, H, R, F, Fs, FML, FMR, FRL, FRR, Vx, Vy, Vxs, Vys, DO,
+    G, G2, H, R, F, Fs, FM, FR, Vx, Vy, Vxs, Vys, DO,
     dest, gid, DML, DMR, DRL, DRR, lsem, ssem, rsem,
 ):
     X, St = (XA, XB), (SA, SB)
@@ -75,7 +75,8 @@
     at_left, at_right = iy == 0, iy == ny - 1
 
     barrier = pltpu.get_barrier_semaphore()
-    greet = [(xs[dx], ys[dy], ig) for dx, dy in around] + [partner] + z_peer[1:]
+    greet = [(xs[dx], ys[dy], 2 * z + c) for dx, dy in around for c in (0, 1)]
+    greet += [partner] + z_peer[1:]
     for device in greet:
         pl.semaphore_signal(barrier, inc=1, device_id=device, device_id_type=MESH)
 
@@ -235,7 +236,14 @@
             strip_row[side] = jnp.where(here, row, strip_row[side])
 
     def relax(centre, up, down, left, right, s):
-        return soft_min([centre, up + s, down + s, left + s, right + s], K_SWEEP, SWEEP_TEMP)
+        beside = (up, down, left, right)
+        near = jnp.minimum(jnp.minimum(up, down), jnp.minimum(left, right))
+        least = jnp.minimum(centre, near + s)
+        total = jnp.exp2((least - centre) * K_SWEEP)
+        level = least - s
+        for item in beside:
+            total += jnp.exp2((level - item) * K_SWEEP)
+        return least - SWEEP_TEMP * jnp.log(total)
 
     def three(base):
         return tile_at(base), pl.ds(base - 1, 8), pl.ds(base + 1, 8)
@@ -482,14 +490,53 @@
 
     def build_field(i):
         t = tile_at(PAD - 8 + 8 * i)
-        f = jnp.where(own_left, in_slots([F[k, 0, t] for k in range(groups)], 8), FRL[t])
+        f = jnp.where(own_left, in_slots([F[k, 0, t] for k in range(groups)], 8), FR[0, t])
         Fs[0, t] = jnp.where(at_left & ~own_left, roll(f, -1), f)
         f = jnp.where(
-            own_right, in_slots([F[k, halves - 1, t] for k in range(groups)], 24 - LANES), FRR[t]
+            own_right, in_slots([F[k, halves - 1, t] for k in range(groups)], 24 - LANES), FR[1, t]
         )
         Fs[1, t] = jnp.where(at_right & ~own_right, roll(f, 1), f)
 
-    pack_field = pack_columns(F, FMR, FML)
+    toward = lax.rem(iy + ny - 1 + 2 * core, ny)
+    shift = 24 - 16 * core
+
+    def pack_field(i):
+        t = tile_at(PAD + 8 * i)
+        out = pltpu.roll(F[0, core, t], shift, 1)
+        for k in range(1, groups):
+            out = jnp.where(slot == k, pltpu.roll(F[k, core, t], shift + 32 * k, 1), out)
+        FM[tile_at(8 * i)] = out
+
+    class Both:
+        def __init__(self, src, dst_of, x, y):
+            base = sent[0]
+            sent[0] += 2
+            self.sends, self.receipts = [], []
+            for c in (0, 1):
+                copy = pltpu.make_async_remote_copy(
+                    src_ref=src, dst_ref=dst_of(core),
+                    send_sem=ssem.at[base + c], recv_sem=rsem.at[base + core],
+                    device_id=(x, y, 2 * z + c), device_id_type=MESH,
+                )
+                copy.start()
+                self.sends.append(copy)
+                self.receipts.append(
+                    pltpu.make_async_remote_copy(
+                        src_ref=src, dst_ref=dst_of(c),
+                        send_sem=ssem.at[base + c], recv_sem=rsem.at[base + c],
+                        device_id=(x, y, 2 * z + c), device_id_type=MESH,
+                    )
+                )
+
+        def wait(self):
+            for copy in self.receipts:
+                copy.wait_recv()
+            for copy in self.sends:
+                copy.wait_send()
+
+    def columns(rows):
+        return lambda c: FR.at[1 - c, rows]
+
     halos = []
 
     def collect(q):
@@ -497,16 +544,15 @@
         for d in order[::-1]:
             gather[q][d].wait_recv()
             arrived.append(remote(mine(q, z_back[d]), mine(q, z_back[d]), partner))
+        dx, here, there, row = ((-1, first, below, p_first), (1, last, above, p_last))[q]
+        loop(tiles * q, tiles * (q + 1), pack_field, unroll=4)
+        side = pl.ds(part * q, part), pl.ds(PAD + part * q, part)
+        out = [Both(FM.at[side[0]], columns(side[1]), ix, toward)]
+        out.append(Both(FM.at[here], columns(there), xs[dx], toward))
+        out.append(Both(F.at[:, core, row], lambda c: F.at[:, c, there], xs[dx], iy))
+        halos.append(out)
         for copy in [forward[q]] + arrived:
             copy.wait_recv()
-        loop(tiles * q, tiles * (q + 1), pack_field, unroll=4)
-        if q == 0:
-            out = [remote(F.at[:, :, p_first], F.at[:, :, below], north)]
-            out += send_corners(FMR, FML, FRL, FRR, -1)
-        else:
-            out = [remote(F.at[:, :, p_last], F.at[:, :, above], south)]
-            out += send_corners(FMR, FML, FRL, FRR, 1)
-        halos.append(out + send_sides(FMR, FML, FRL, FRR, part * q, part))
         return arrived
 
     passed = collect(0)
@@ -586,7 +632,7 @@
             vm(groups, halves, *panel), vm(2, *panel), vm(*flat), vm(*flat), vm(*panel), vm(*panel),
             vm(groups, halves, *flat), vm(groups, *flat), vm(groups, *flat),
             vm(2, nz, groups, height // (2 * nz), LANES), vm(groups, halves, *panel), vm(2, *panel),
-            vm(*flat), vm(*flat), vm(*panel), vm(*panel),
+            vm(*flat), vm(2, *panel),
             vm(groups, halves, *panel), vm(groups, halves, *panel), vm(2, *panel), vm(2, *panel),
             vm(groups, halves, *flat),
             pltpu.SMEM((goals,), jnp.int32), pltpu.SMEM((goals,), jnp.int32),

time: 51 us -> 51 us (level)
  no operation moved by 1% of the time
where the time goes in v5:
time: 51 us; the launch traced here: 50.9 us
  Pallas kernels  50.3 us (99%)
  between operations  0.64 us (1%)
    pallas_call x1, Pallas kernels, per_device(): pl.pallas_call(functools.partial(kernel, nx, ny, nz, goals, groups, heigh...  48.9 us
    pallas_call x1, Pallas kernels, per_device(): pl.pallas_call(settle, out_shape=tuple((jax.ShapeDtypeStruct(r.shape, f32...  1.34 us

profile of v5, /device:TPU:1, one launch (start us, length us, event | category | flops | bytes accessed | tf_op | source)
XLA Modules:
  0.0 50.9 jit_solution(14913088930538681407)
XLA Ops:
  0.6 48.9 %crowd_step.1 = (f32[4,128,256]{2,1,0:T(8,128)S(1)}, f32[4,2,128,256]{3,2,1,0:T(8,128)S(1)}, f32[4,128,256]{2,1,0:T(8,128)S(1)}) custom-call(f32[4,128,256]{2,1,0:T(8,128)} %pot.1, f32[128,256]{1,0:T(8,128)} %cost.1, s32[128,256]{1,0:T(8,128)} %obst.1, f32[4,128,256]{2,1,0:T(8,128)} %dens.1, s32[4]{0:T(128)} %dest_in.1, s32[4]{0:T(128)} %gid_in.1), custom_call_target="tpu_custom_call" | custom-call | tf_op jit(solution)/shard_map/crowd_step/pallas_call | solution.py:645
  49.6 1.3 %settle.1 = (f32[4,128,256]{2,1,0:T(8,128)}, f32[4,2,128,256]{3,2,1,0:T(8,128)}, f32[4,128,256]{2,1,0:T(8,128)}) custom-call(f32[4,128,256]{2,1,0:T(8,128)S(1)} %get-tuple-element.6.refs_0_, f32[4,2,128,256]{3,2,1,0:T(8,128)S(1)} %get-tuple-element.7.refs_1_, f32[4,128,256]{2,1,0:T(8,128)S(1)} %get-tuple-element.8.refs_2_), custom_call_target="tpu_custom_call" | custom-call | tf_op jit(solution)/shard_map/settle/pallas_call | solution.py:660

commit v6 on v5

--- a/solution.py
+++ b/solution.py
@@ -385,6 +385,7 @@
     def mine(q, j):
         return F.at[:, core, pl.ds(pl.multiple_of(PAD + part * q + chunk * j, 8), chunk)]
 
+    near = [2, nz - 2, 1, nz - 1] if nz == 8 else order
     for q in range(parts):
         for copy in spread[q]:
             copy.wait_recv()
@@ -394,7 +395,8 @@
                 items = [H[k, tile_at(row)]]
                 items += [R[q, d, k, 8 * i : 8 * i + 8] for d in range(1, nz)]
                 F[k, core, tile_at(PAD + row)] = soft_min(items, K_GOAL, GOAL_TEMP)
-        gather.append({d: remote(mine(q, z), mine(q, z), z_peer[d]) for d in order})
+        reach = near if q == 0 else order
+        gather.append({d: remote(mine(q, z), mine(q, z), z_peer[d]) for d in reach})
         forward.append(remote(mine(q, z), mine(q, z), partner))
 
     inv_two_cells = 1.0 / (2.0 * CELL_SIZE)
@@ -540,9 +542,21 @@
     halos = []
 
     def collect(q):
-        arrived = []
-        for d in order[::-1]:
-            gather[q][d].wait_recv()
+        arrived, relays = [], {}
+        if q == 0 and nz == 8:
+            gather[0][2].wait_recv()
+            gather[0][nz - 2].wait_recv()
+            step = 2 + (nz - 4) * core
+            source, target = lax.rem(z + nz - step, nz), lax.rem(z + step, nz)
+            relays[4] = remote(mine(0, source), mine(0, source), (ix, iy, 2 * target + core))
+            relays[3] = remote(mine(0, z_back[2]), mine(0, z_back[2]), z_peer[1])
+            back = mine(0, z_back[nz - 2])
+            relays[nz - 3] = remote(back, back, z_peer[nz - 1])
+        for d in (near + list(relays)) if relays else order[::-1]:
+            if d in relays:
+                relays[d].wait_recv()
+            elif not (relays and d in (2, nz - 2)):
+                gather[q][d].wait_recv()
             arrived.append(remote(mine(q, z_back[d]), mine(q, z_back[d]), partner))
         dx, here, there, row = ((-1, first, below, p_first), (1, last, above, p_last))[q]
         loop(tiles * q, tiles * (q + 1), pack_field, unroll=4)
@@ -553,7 +567,7 @@
         halos.append(out)
         for copy in [forward[q]] + arrived:
             copy.wait_recv()
-        return arrived
+        return arrived + list(relays.values())
 
     passed = collect(0)
     loop(2, 8, flows, unroll=2)

time: 51 us -> 52.9 us (1.037)
  Pallas kernels: 50.3 us -> 52.2 us
    pallas_call x1, Pallas kernels: 48.9 us -> 50.8 us  [per_device(): pl.pallas_call(functools.partial(kernel, nx, ny, nz, goals, groups, heigh...]
where the time goes in v6:
time: 52.9 us; the launch traced here: 52.8 us
  Pallas kernels  52.2 us (99%)
  between operations  0.64 us (1%)
    pallas_call x1, Pallas kernels, per_device(): pl.pallas_call(functools.partial(kernel, nx, ny, nz, goals, groups, heigh...  50.8 us
    pallas_call x1, Pallas kernels, per_device(): pl.pallas_call(settle, out_shape=tuple((jax.ShapeDtypeStruct(r.shape, f32...  1.34 us

profile of v6, /device:TPU:1, one launch (start us, length us, event | category | flops | bytes accessed | tf_op | source)
XLA Modules:
  0.0 52.8 jit_solution(7075624013126884102)
XLA Ops:
  0.6 50.8 %crowd_step.1 = (f32[4,128,256]{2,1,0:T(8,128)S(1)}, f32[4,2,128,256]{3,2,1,0:T(8,128)S(1)}, f32[4,128,256]{2,1,0:T(8,128)S(1)}) custom-call(f32[4,128,256]{2,1,0:T(8,128)} %pot.1, f32[128,256]{1,0:T(8,128)} %cost.1, s32[128,256]{1,0:T(8,128)} %obst.1, f32[4,128,256]{2,1,0:T(8,128)} %dens.1, s32[4]{0:T(128)} %dest_in.1, s32[4]{0:T(128)} %gid_in.1), custom_call_target="tpu_custom_call" | custom-call | tf_op jit(solution)/shard_map/crowd_step/pallas_call | solution.py:659
  51.5 1.3 %settle.1 = (f32[4,128,256]{2,1,0:T(8,128)}, f32[4,2,128,256]{3,2,1,0:T(8,128)}, f32[4,128,256]{2,1,0:T(8,128)}) custom-call(f32[4,128,256]{2,1,0:T(8,128)S(1)} %get-tuple-element.6.refs_0_, f32[4,2,128,256]{3,2,1,0:T(8,128)S(1)} %get-tuple-element.7.refs_1_, f32[4,128,256]{2,1,0:T(8,128)S(1)} %get-tuple-element.8.refs_2_), custom_call_target="tpu_custom_call" | custom-call | tf_op jit(solution)/shard_map/settle/pallas_call | solution.py:674
